TPU v7x, 256 devices: a whole 4x4x8 slice. The times are simulated.
256 devices in a mesh: hel: 16 (over x_hi, z), rad: 16 (over x_lo, y, core).
Axes of the slice: x: 4 (x_hi: 2, x_lo: 2; x = x_hi * 2 + x_lo), y: 4, z: 8, core: 2. Of those that a mesh axis runs over, the one named last changes fastest.
Arguments:
- psi_start: float32 [16, 256, 16, 768], P('hel', 'rad'), may hold values from -6 to 6
- potential: float32 [256, 16, 1536], P('rad'), may hold values from -0.5 to 0.5
- basis: bfloat16 [768, 1536], replicated, may hold values from -0.21875 to 0.21875
- kinetic: bfloat16 [256, 256], replicated, may hold values from -0.375 to 0.375
- radial_factor: float32 [256], P('rad'), may hold values from 0.002 to 0.02
- damping: float32 [256], P('rad'), may hold values from 0.7 to 1
- coupling: bfloat16 [16, 768], P('hel'), may hold values from -2 to 2
- helicity: int32 [16], P('hel'), may hold values from 0 to 7
- chan_rad: int32 [1024], replicated, may hold values from 0 to 255
- chan_vib: int32 [1024], replicated, may hold values from 0 to 15
- projector: bfloat16 [1024, 768], replicated, may hold values from -0.21875 to 0.21875
Outputs:
- psi_final: float32 [16, 256, 16, 768], P('hel', 'rad')
- amplitude: float32 [16, 1024], P('hel', 'rad')
All inputs are finite; a program needn't handle non-finite values.
Results may differ from a plain program's by a relative error of at most 0.0046.
Values may be sent and summed in bfloat16 or wider, within the bound.
A program may use at most 64 MiB of HBM per device.

v0:
```python
import jax
import jax.numpy as jnp
from jax import lax
from jax.sharding import PartitionSpec as P

ITERS = 3


def from_behind(block, axis, distance):
    devices = range(lax.axis_size(axis))
    route = [(i - distance, i) for i in devices if i - distance in devices]
    return lax.ppermute(block, axis, route)


def cut_along(value, dim, count):
    before, after = (value.shape[:dim], value.shape[dim + 1 :])
    return jnp.moveaxis(value.reshape(*before, count, -1, *after), dim, 0)


def sent_and_summed(value, axis, dim):
    tiles = cut_along(value, dim, lax.axis_size(axis))
    arrived = lax.all_to_all(tiles, axis, split_axis=0, concat_axis=0, tiled=True)
    return arrived.sum(axis=0)


def per_device(
    psi_start,
    potential,
    basis,
    kinetic,
    radial_factor,
    damping,
    coupling,
    helicity,
    chan_rad,
    chan_vib,
    projector,
):
    hdev, rdev, nvib, nang = psi_start.shape
    nquad = basis.shape[1]
    rad_index = lax.axis_index("rad")
    hel_index = lax.axis_index("hel")
    total_blocks = lax.axis_size("hel") * hdev
    block_ids = hel_index * hdev + jnp.arange(hdev, dtype=jnp.int32)
    coupling_eff = jnp.where(
        (block_ids < total_blocks - 1)[:, None], coupling, jnp.zeros_like(coupling)
    )
    kvalue = helicity.astype(jnp.float32)
    pot_rows = potential.reshape(1, -1, nquad)
    damp = damping[None, :, None, None]

    def ham(psi):
        packed = psi.astype(jnp.bfloat16)
        lower_pb, lower_cp = from_behind((packed, coupling_eff), "hel", 1)
        upper_pb = from_behind(packed, "hel", -1)
        regrouped = lax.all_to_all(packed, "rad", split_axis=2, concat_axis=1, tiled=True)
        kin_moved = jnp.einsum(
            "rs,ksvj->krvj", kinetic, regrouped, preferred_element_type=jnp.float32
        )
        kin = lax.all_to_all(kin_moved, "rad", split_axis=1, concat_axis=2, tiled=True)
        grid = jnp.dot(packed.reshape(-1, nang), basis, preferred_element_type=jnp.float32)
        scaled = (grid.reshape(hdev, -1, nquad) * pot_rows).astype(jnp.bfloat16)
        ang = lax.dot_general(
            scaled.reshape(-1, nquad),
            basis,
            (((1,), (1,)), ((), ())),
            preferred_element_type=jnp.float32,
        )
        ang = ang.reshape(psi.shape)
        upper = jnp.concatenate([packed[1:], upper_pb], axis=0).astype(jnp.float32)
        lower = jnp.concatenate([lower_pb, packed[:-1]], axis=0).astype(jnp.float32)
        coupling_prev = jnp.concatenate([lower_cp, coupling_eff[:-1]], axis=0).astype(jnp.float32)
        cor = (
            coupling_eff.astype(jnp.float32)[:, None, None, :] * upper
            + coupling_prev[:, None, None, :] * lower
        )
        cen = (
            -2.0 * (kvalue * kvalue)[:, None, None, None] * radial_factor[None, :, None, None] * psi
        )
        return kin + ang + cen + cor

    previous = psi_start
    current = damp * ham(psi_start)
    for step in range(ITERS - 1):
        following = damp * (2.0 * ham(current) - damp * previous)
        previous, current = (current, following)
    final_b = current.astype(jnp.bfloat16)
    local_rad = chan_rad - rad_index * rdev
    inside = (local_rad >= 0) & (local_rad < rdev)
    slot = jnp.where(inside, local_rad * nvib + chan_vib, -1)
    select = (slot[:, None] == jnp.arange(rdev * nvib, dtype=jnp.int32)[None, :]).astype(
        jnp.bfloat16
    )
    rows = jnp.einsum(
        "cq,kqj->kcj",
        select,
        final_b.reshape(hdev, rdev * nvib, nang),
        preferred_element_type=jnp.float32,
    )
    partial_amp = jnp.sum(rows * projector.astype(jnp.float32)[None], axis=-1)
    amplitude = sent_and_summed(partial_amp, "rad", 1)
    return (current, amplitude)


def solution(mesh):
    placed = (
        P("hel", "rad", None, None),
        P("rad", None, None),
        P(),
        P(),
        P("rad"),
        P("rad"),
        P("hel", None),
        P("hel"),
        P(),
        P(),
        P(),
    )
    return jax.shard_map(
        per_device,
        mesh=mesh,
        in_specs=placed,
        out_specs=(P("hel", "rad", None, None), P("hel", "rad")),
        check_vma=False,
    )
```

profile of v0, /device:TPU:5, one launch (start us, length us, event | category | flops | bytes accessed | tf_op | source)
XLA Modules:
  0.0 158.3 jit_solution(11509767006153960879)
XLA Ops:
  0.6 1.3 convert_element_type.53
  2.0 0.9 copy.45
  2.8 5.8 %all-to-all-start = ((bf16[1,16,16,768]{3,1,0,2:T(8,128)(2,1)}), bf16[1,16,16,768]{3,1,0,2:T(8,128)(2,1)}, u32[]{:S(2)}, u32[]{:S(2)}) async-start(bf16[1,16,16,768]{3,1,0,2:T(8,128)(2,1)} %copy.45), calls=%async_computation | async-start | bytes 786432 | tf_op jit(solution)/shard_map/all_to_all | solution.py:56
  8.6 7.7 %collective-permute-start = (bf16[1,16,16,768]{3,2,1,0:T(8,128)(2,1)S(1)}, bf16[1,16,16,768]{3,2,1,0:T(8,128)(2,1)S(1)}, u32[]{:S(2)}, u32[]{:S(2)}) collective-permute-start(bf16[1,16,16,768]{3,2,1,0:T(8,128)(2,1)S(1)} %convert_element_type.53), channel_id=1, source_target_pairs={{16,0},{32,16},{48,32},{64,48},{80,64},{96,80},{112,96},{128,112},... | collective-permute-start | bytes 1179656 | tf_op jit(solution)/shard_map/ppermute | solution.py:12
  16.4 1.9 %collective-permute-start.2 = (bf16[1,16,16,768]{3,2,1,0:T(8,128)(2,1)S(1)}, bf16[1,16,16,768]{3,2,1,0:T(8,128)(2,1)S(1)}, u32[]{:S(2)}, u32[]{:S(2)}) collective-permute-start(bf16[1,16,16,768]{3,2,1,0:T(8,128)(2,1)S(1)} %convert_element_type.53), channel_id=1, source_target_pairs={{0,16},{16,32},{32,48},{48,64},{64,80},{80,96},{96,112},{112,128},... | collective-permute-start | bytes 1179656 | tf_op jit(solution)/shard_map/ppermute | solution.py:12
  18.3 2.2 %convolution_bitcast_fusion.2 = f32[1,256,1,768]{1,3,2,0:T(8,128)} fusion(bf16[256,768]{1,0:T(8,128)(2,1)} %bitcast.2, bf16[256,256]{1,0:T(8,128)(2,1)} %param.14), kind=kOutput, calls=%fused_computation.22 | convolution fusion | flops 100663296 | bytes 1310720 | tf_op jit(solution)/shard_map/rs,ksvj->krvj/dot_general | solution.py:57
  20.5 3.1 %copy.46 = f32[1,256,1,768]{3,2,0,1:T(1,128)} copy(f32[1,256,1,768]{1,3,2,0:T(8,128)} %convolution_bitcast_fusion.2) | data formatting | bytes 1572864 | tf_op jit(solution)/shard_map/rs,ksvj->krvj/transpose | solution.py:57
  23.6 6.6 %all-to-all-start.1 = ((f32[1,256,1,768]{3,2,0,1:T(1,128)}), f32[1,256,1,768]{3,2,0,1:T(1,128)}, u32[]{:S(2)}, u32[]{:S(2)}) async-start(f32[1,256,1,768]{3,2,0,1:T(1,128)} %copy.46), calls=%async_computation.1 | async-start | bytes 1572864 | tf_op jit(solution)/shard_map/all_to_all | solution.py:60
  30.2 1.9 %collective-permute-start.1 = (bf16[1,768]{1,0:T(2,128)(2,1)S(1)}, bf16[1,768]{1,0:T(2,128)(2,1)S(1)}, u32[]{:S(2)}, u32[]{:S(2)}) collective-permute-start(bf16[1,768]{1,0:T(2,128)(2,1)S(1)} %get-tuple-element.3), channel_id=1, source_target_pairs={{0,16},{16,32},{32,48},{48,64},{64,80},{80,96},{96,112},{112,128},... | collective-permute-start | bytes 4616 | tf_op jit(solution)/shard_map/ppermute | solution.py:12
  32.2 3.1 %fusion.1 = bf16[256,1536]{1,0:T(8,128)(2,1)} fusion(f32[256,1536]{1,0:T(8,128)} %bitcast.131, bf16[256,768]{1,0:T(8,128)(2,1)S(1)} %bitcast.136, bf16[768,1536]{1,0:T(8,128)(2,1)S(1)} %copy-done), kind=kOutput, calls=%fused_computation.5 | convolution fusion | flops 604766208 | bytes 5111808 | tf_op jit(solution)/shard_map/dot_general | solution.py:61
  35.9 2.3 %collective-permute-done.1 = bf16[1,768]{1,0:T(2,128)(2,1)S(1)} collective-permute-done((bf16[1,768]{1,0:T(2,128)(2,1)S(1)}, bf16[1,768]{1,0:T(2,128)(2,1)S(1)}, u32[]{:S(2)}, u32[]{:S(2)}) %collective-permute-start.1) | collective-permute-done | bytes 1568 | tf_op jit(solution)/shard_map/ppermute | solution.py:12
  38.3 5.0 %all-to-all-done.1 = f32[1,256,1,768]{3,2,0,1:T(1,128)} async-done(((f32[1,256,1,768]{3,2,0,1:T(1,128)}), f32[1,256,1,768]{3,2,0,1:T(1,128)}, u32[]{:S(2)}, u32[]{:S(2)}) %all-to-all-start.1) | async-done | bytes 786464 | tf_op jit(solution)/shard_map/all_to_all | solution.py:60
  43.3 1.2 copy.56
  44.5 0.7 copy-done.1
  45.3 2.8 %fusion.41 = (bf16[1,16,16,768]{3,2,1,0:T(8,128)(2,1)S(1)}, f32[1,16,16,768]{3,2,1,0:T(8,128)S(1)}) fusion(bf16[1,16,16,768]{3,2,1,0:T(8,128)(2,1)} %copy-done.1, bf16[1,16,16,768]{3,2,1,0:T(8,128)(2,1)S(1)} %collective-permute-done, f32[768]{0:T(1024)S(1)} %convert_reduce_fusion, f32[768]{0:T(1024)S(1)} %get-tuple-element.2, f32[16]{0:T(128)S(1)} %copy-done.7, ...), kind=kOutput, calls=%fused_computation.30 | convolution fusion | flops 606142464 | bytes 6690944 | tf_op jit(solution)/shard_map/dot_general | solution.py:63
  48.0 0.8 copy-done.3
  48.8 0.1 copy.48
  48.9 11.8 %all_to_all.104 = bf16[1,16,16,768]{3,1,0,2:T(8,128)(2,1)S(1)} all-to-all(bf16[1,16,16,768]{3,1,0,2:T(8,128)(2,1)S(1)} %copy.48), channel_id=1, replica_groups=mesh['hel'=16,'rad'=16] {'rad'}, dimensions={2} | all-to-all | bytes 786432 | tf_op jit(solution)/shard_map/all_to_all | solution.py:56
  60.7 1.2 convolution_bitcast_fusion.1
  61.9 3.1 %copy.49 = f32[1,256,1,768]{3,2,0,1:T(1,128)} copy(f32[1,256,1,768]{1,3,2,0:T(8,128)} %convolution_bitcast_fusion.1) | data formatting | bytes 1572864 | tf_op jit(solution)/shard_map/rs,ksvj->krvj/transpose | solution.py:57
  64.9 5.2 %all-to-all-start.3 = ((f32[1,256,1,768]{3,2,0,1:T(1,128)}), f32[1,256,1,768]{3,2,0,1:T(1,128)}, u32[]{:S(2)}, u32[]{:S(2)}) async-start(f32[1,256,1,768]{3,2,0,1:T(1,128)} %copy.49), calls=%async_computation.3 | async-start | bytes 1572864 | tf_op jit(solution)/shard_map/all_to_all | solution.py:60
  70.1 6.6 %collective-permute-start.3 = (bf16[1,16,16,768]{3,2,1,0:T(8,128)(2,1)}, bf16[1,16,16,768]{3,2,1,0:T(8,128)(2,1)}, u32[]{:S(2)}, u32[]{:S(2)}) collective-permute-start(bf16[1,16,16,768]{3,2,1,0:T(8,128)(2,1)} %copy-done.3), channel_id=1, source_target_pairs={{16,0},{32,16},{48,32},{64,48},{80,64},{96,80},{112,96},{128,112},... | collective-permute-start | bytes 1179656 | tf_op jit(solution)/shard_map/ppermute | solution.py:12
  76.8 1.9 %collective-permute-start.4 = (bf16[1,16,16,768]{3,2,1,0:T(8,128)(2,1)}, bf16[1,16,16,768]{3,2,1,0:T(8,128)(2,1)}, u32[]{:S(2)}, u32[]{:S(2)}) collective-permute-start(bf16[1,16,16,768]{3,2,1,0:T(8,128)(2,1)} %copy-done.3), channel_id=1, source_target_pairs={{0,16},{16,32},{32,48},{48,64},{64,80},{80,96},{96,112},{112,128},... | collective-permute-start | bytes 1179656 | tf_op jit(solution)/shard_map/ppermute | solution.py:12
  78.7 3.2 %fusion.2 = bf16[256,1536]{1,0:T(8,128)(2,1)} fusion(f32[256,1536]{1,0:T(8,128)} %bitcast.132, bf16[256,768]{1,0:T(8,128)(2,1)} %bitcast.135, bf16[768,1536]{1,0:T(8,128)(2,1)S(1)} %copy-done), kind=kOutput, calls=%fused_computation.6 | convolution fusion | flops 604766208 | bytes 5111808 | tf_op jit(solution)/shard_map/dot_general | solution.py:61
  81.9 1.4 all-to-all-done.3
  83.3 1.2 copy.57
  84.5 0.9 collective-permute-done.3
  85.3 7.4 %collective-permute-done.4 = bf16[1,16,16,768]{3,2,1,0:T(8,128)(2,1)} collective-permute-done((bf16[1,16,16,768]{3,2,1,0:T(8,128)(2,1)}, bf16[1,16,16,768]{3,2,1,0:T(8,128)(2,1)}, u32[]{:S(2)}, u32[]{:S(2)}) %collective-permute-start.4) | collective-permute-done | bytes 393248 | tf_op jit(solution)/shard_map/ppermute | solution.py:12
  92.7 4.1 %fusion.43 = (bf16[1,16,16,768]{3,2,1,0:T(8,128)(2,1)S(1)}, f32[1,16,16,768]{3,2,1,0:T(8,128)}) fusion(f32[1,16,16,768]{3,2,1,0:T(8,128)} %param.11, bf16[1,16,16,768]{3,2,1,0:T(8,128)(2,1)} %collective-permute-done.4, bf16[1,16,16,768]{3,2,1,0:T(8,128)(2,1)} %collective-permute-done.3, f32[1,16,16,768]{3,2,1,0:T(8,128)S(1)} %get-tuple-element.5, ...), kind=kOutput, calls=%fused_computation.37 | convolution fusion | flops 608108544 | bytes 8263808 | tf_op jit(solution)/shard_map/dot_general | solution.py:63
  96.8 0.8 copy-done.2
  97.5 0.1 copy.51
  97.7 15.7 %all_to_all.105 = bf16[1,16,16,768]{3,1,0,2:T(8,128)(2,1)S(1)} all-to-all(bf16[1,16,16,768]{3,1,0,2:T(8,128)(2,1)S(1)} %copy.51), channel_id=1, replica_groups=mesh['hel'=16,'rad'=16] {'rad'}, dimensions={2} | all-to-all | bytes 786432 | tf_op jit(solution)/shard_map/all_to_all | solution.py:56
  113.3 1.2 convolution_bitcast_fusion
  114.5 3.0 %copy.52 = f32[1,256,1,768]{3,2,0,1:T(1,128)} copy(f32[1,256,1,768]{1,3,2,0:T(8,128)} %convolution_bitcast_fusion) | data formatting | bytes 1572864 | tf_op jit(solution)/shard_map/rs,ksvj->krvj/transpose | solution.py:57
  117.5 5.2 %all-to-all-start.5 = ((f32[1,256,1,768]{3,2,0,1:T(1,128)}), f32[1,256,1,768]{3,2,0,1:T(1,128)}, u32[]{:S(2)}, u32[]{:S(2)}) async-start(f32[1,256,1,768]{3,2,0,1:T(1,128)} %copy.52), calls=%async_computation.5 | async-start | bytes 1572864 | tf_op jit(solution)/shard_map/all_to_all | solution.py:60
  122.7 1.9 %collective-permute-start.5 = (bf16[1,16,16,768]{3,2,1,0:T(8,128)(2,1)}, bf16[1,16,16,768]{3,2,1,0:T(8,128)(2,1)}, u32[]{:S(2)}, u32[]{:S(2)}) collective-permute-start(bf16[1,16,16,768]{3,2,1,0:T(8,128)(2,1)} %copy-done.2), channel_id=1, source_target_pairs={{16,0},{32,16},{48,32},{64,48},{80,64},{96,80},{112,96},{128,112},... | collective-permute-start | bytes 1179656 | tf_op jit(solution)/shard_map/ppermute | solution.py:12
  124.7 3.4 %collective-permute-start.6 = (bf16[1,16,16,768]{3,2,1,0:T(8,128)(2,1)}, bf16[1,16,16,768]{3,2,1,0:T(8,128)(2,1)}, u32[]{:S(2)}, u32[]{:S(2)}) collective-permute-start(bf16[1,16,16,768]{3,2,1,0:T(8,128)(2,1)} %copy-done.2), channel_id=1, source_target_pairs={{0,16},{16,32},{32,48},{48,64},{64,80},{80,96},{96,112},{112,128},... | collective-permute-start | bytes 1179656 | tf_op jit(solution)/shard_map/ppermute | solution.py:12
  128.0 1.3 add_select_fusion
  129.3 2.6 %copy.54 = bf16[1024,768]{0,1:T(8,128)(2,1)} copy(bf16[1024,768]{1,0:T(8,128)(2,1)} %param.21) | data formatting | bytes 3145728 | tf_op args[10]
  131.9 3.2 %fusion.3 = bf16[256,1536]{1,0:T(8,128)(2,1)} fusion(f32[256,1536]{1,0:T(8,128)} %bitcast.133, bf16[256,768]{1,0:T(8,128)(2,1)} %bitcast.134, bf16[768,1536]{1,0:T(8,128)(2,1)S(1)} %copy-done), kind=kOutput, calls=%fused_computation.7 | convolution fusion | flops 604766208 | bytes 5111808 | tf_op jit(solution)/shard_map/dot_general | solution.py:61
  135.1 0.8 all-to-all-done.5
  135.9 1.2 copy.58
  137.1 3.8 %collective-permute-done.6 = bf16[1,16,16,768]{3,2,1,0:T(8,128)(2,1)} collective-permute-done((bf16[1,16,16,768]{3,2,1,0:T(8,128)(2,1)}, bf16[1,16,16,768]{3,2,1,0:T(8,128)(2,1)}, u32[]{:S(2)}, u32[]{:S(2)}) %collective-permute-start.6) | collective-permute-done | bytes 393248 | tf_op jit(solution)/shard_map/ppermute | solution.py:12
  140.9 4.1 %fusion.44 = (bf16[1,16,16,768]{3,2,1,0:T(8,128)(2,1)S(1)}, f32[1,16,16,768]{3,2,1,0:T(8,128)}) fusion(f32[1,16,16,768]{3,2,1,0:T(8,128)S(1)} %get-tuple-element.5, bf16[1,16,16,768]{3,2,1,0:T(8,128)(2,1)} %copy-done.1, bf16[1,16,16,768]{3,2,1,0:T(8,128)(2,1)S(1)} %collective-permute-done, bf16[1,16,16,768]{3,2,1,0:T(8,128)(2,1)} %collective-permute-done.6, ...), kind=kOutput, calls=%fused_computation.38 | convolution fusion | flops 608108544 | bytes 8263808 | tf_op jit(solution)/shard_map/dot_general | solution.py:63
  145.1 0.8 fusion
  145.9 0.1 transpose_reshape.3
  146.0 11.8 %all_to_all.106 = f32[16,1,64]{2,1,0:T(1,128)S(1)} all-to-all(f32[16,1,64]{2,1,0:T(1,128)S(1)} %transpose_reshape.3), channel_id=1, replica_groups=mesh['hel'=16,'rad'=16] {'rad'}, dimensions={0} | all-to-all | bytes 8192 | tf_op jit(solution)/shard_map/all_to_all | solution.py:22
  157.8 0.5 reduce_sum.21
  (26 shorter events, 0.1 us)
Async XLA Ops:
  0.6 31.5 %copy-start = (bf16[768,1536]{1,0:T(8,128)(2,1)S(1)}, bf16[768,1536]{1,0:T(8,128)(2,1)}, u32[]{:S(2)}) copy-start(bf16[768,1536]{1,0:T(8,128)(2,1)} %param.13) | copy-start | bytes 7077892
  2.8 15.5 %all-to-all-start = ((bf16[1,16,16,768]{3,1,0,2:T(8,128)(2,1)}), bf16[1,16,16,768]{3,1,0,2:T(8,128)(2,1)}, u32[]{:S(2)}, u32[]{:S(2)}) async-start(bf16[1,16,16,768]{3,1,0,2:T(8,128)(2,1)} %copy.45), calls=%async_computation | async-start | bytes 786432 | tf_op jit(solution)/shard_map/all_to_all | solution.py:56
  8.6 21.6 %copy-start.9 = (bf16[1,768]{1,0:T(2,128)(2,1)S(1)}, bf16[1,768]{1,0:T(2,128)(2,1)}, u32[]{:S(2)}) copy-start(bf16[1,768]{1,0:T(2,128)(2,1)} %param.17) | copy-start | bytes 4612
  8.6 35.8 %collective-permute-start = (bf16[1,16,16,768]{3,2,1,0:T(8,128)(2,1)S(1)}, bf16[1,16,16,768]{3,2,1,0:T(8,128)(2,1)S(1)}, u32[]{:S(2)}, u32[]{:S(2)}) collective-permute-start(bf16[1,16,16,768]{3,2,1,0:T(8,128)(2,1)S(1)} %convert_element_type.53), channel_id=1, source_target_pairs={{16,0},{32,16},{48,32},{64,48},{80,64},{96,80},{112,96},{128,112},... | collective-permute-start | bytes 1179656 | tf_op jit(solution)/shard_map/ppermute | solution.py:12
  16.4 28.1 %collective-permute-start.2 = (bf16[1,16,16,768]{3,2,1,0:T(8,128)(2,1)S(1)}, bf16[1,16,16,768]{3,2,1,0:T(8,128)(2,1)S(1)}, u32[]{:S(2)}, u32[]{:S(2)}) collective-permute-start(bf16[1,16,16,768]{3,2,1,0:T(8,128)(2,1)S(1)} %convert_element_type.53), channel_id=1, source_target_pairs={{0,16},{16,32},{32,48},{48,64},{64,80},{80,96},{96,112},{112,128},... | collective-permute-start | bytes 1179656 | tf_op jit(solution)/shard_map/ppermute | solution.py:12
  23.6 19.7 %all-to-all-start.1 = ((f32[1,256,1,768]{3,2,0,1:T(1,128)}), f32[1,256,1,768]{3,2,0,1:T(1,128)}, u32[]{:S(2)}, u32[]{:S(2)}) async-start(f32[1,256,1,768]{3,2,0,1:T(1,128)} %copy.46), calls=%async_computation.1 | async-start | bytes 1572864 | tf_op jit(solution)/shard_map/all_to_all | solution.py:60
  30.2 8.1 %collective-permute-start.1 = (bf16[1,768]{1,0:T(2,128)(2,1)S(1)}, bf16[1,768]{1,0:T(2,128)(2,1)S(1)}, u32[]{:S(2)}, u32[]{:S(2)}) collective-permute-start(bf16[1,768]{1,0:T(2,128)(2,1)S(1)} %get-tuple-element.3), channel_id=1, source_target_pairs={{0,16},{16,32},{32,48},{48,64},{64,80},{80,96},{96,112},{112,128},... | collective-permute-start | bytes 4616 | tf_op jit(solution)/shard_map/ppermute | solution.py:12
  32.2 3.8 %copy-start.10 = (f32[16]{0:T(128)S(1)}, f32[16]{0:T(128)}, u32[]{:S(2)}) copy-start(f32[16]{0:T(128)} %param.15) | copy-start | bytes 196
  32.2 13.1 %copy-start.7 = (f32[16]{0:T(128)S(1)}, f32[16]{0:T(128)}, u32[]{:S(2)}) copy-start(f32[16]{0:T(128)} %param.16) | copy-start | bytes 196
  44.5 0.8 copy-start.1
  45.3 15.4 %copy-start.5 = (bf16[256,256]{1,0:T(8,128)(2,1)S(1)}, bf16[256,256]{1,0:T(8,128)(2,1)}, u32[]{:S(2)}) copy-start(bf16[256,256]{1,0:T(8,128)(2,1)} %param.14) | copy-start | bytes 393220
  48.0 0.8 copy-start.3
  64.9 18.4 %all-to-all-start.3 = ((f32[1,256,1,768]{3,2,0,1:T(1,128)}), f32[1,256,1,768]{3,2,0,1:T(1,128)}, u32[]{:S(2)}, u32[]{:S(2)}) async-start(f32[1,256,1,768]{3,2,0,1:T(1,128)} %copy.49), calls=%async_computation.3 | async-start | bytes 1572864 | tf_op jit(solution)/shard_map/all_to_all | solution.py:60
  70.1 15.2 %collective-permute-start.3 = (bf16[1,16,16,768]{3,2,1,0:T(8,128)(2,1)}, bf16[1,16,16,768]{3,2,1,0:T(8,128)(2,1)}, u32[]{:S(2)}, u32[]{:S(2)}) collective-permute-start(bf16[1,16,16,768]{3,2,1,0:T(8,128)(2,1)} %copy-done.3), channel_id=1, source_target_pairs={{16,0},{32,16},{48,32},{64,48},{80,64},{96,80},{112,96},{128,112},... | collective-permute-start | bytes 1179656 | tf_op jit(solution)/shard_map/ppermute | solution.py:12
  76.8 15.9 %collective-permute-start.4 = (bf16[1,16,16,768]{3,2,1,0:T(8,128)(2,1)}, bf16[1,16,16,768]{3,2,1,0:T(8,128)(2,1)}, u32[]{:S(2)}, u32[]{:S(2)}) collective-permute-start(bf16[1,16,16,768]{3,2,1,0:T(8,128)(2,1)} %copy-done.3), channel_id=1, source_target_pairs={{0,16},{16,32},{32,48},{48,64},{64,80},{80,96},{96,112},{112,128},... | collective-permute-start | bytes 1179656 | tf_op jit(solution)/shard_map/ppermute | solution.py:12
  92.7 20.6 %copy-start.6 = (bf16[256,256]{1,0:T(8,128)(2,1)S(1)}, bf16[256,256]{1,0:T(8,128)(2,1)}, u32[]{:S(2)}) copy-start(bf16[256,256]{1,0:T(8,128)(2,1)} %param.14) | copy-start | bytes 393220
  96.8 0.8 copy-start.2
  117.5 18.4 %all-to-all-start.5 = ((f32[1,256,1,768]{3,2,0,1:T(1,128)}), f32[1,256,1,768]{3,2,0,1:T(1,128)}, u32[]{:S(2)}, u32[]{:S(2)}) async-start(f32[1,256,1,768]{3,2,0,1:T(1,128)} %copy.52), calls=%async_computation.5 | async-start | bytes 1572864 | tf_op jit(solution)/shard_map/all_to_all | solution.py:60
  122.7 14.4 %collective-permute-start.5 = (bf16[1,16,16,768]{3,2,1,0:T(8,128)(2,1)}, bf16[1,16,16,768]{3,2,1,0:T(8,128)(2,1)}, u32[]{:S(2)}, u32[]{:S(2)}) collective-permute-start(bf16[1,16,16,768]{3,2,1,0:T(8,128)(2,1)} %copy-done.2), channel_id=1, source_target_pairs={{16,0},{32,16},{48,32},{64,48},{80,64},{96,80},{112,96},{128,112},... | collective-permute-start | bytes 1179656 | tf_op jit(solution)/shard_map/ppermute | solution.py:12
  124.7 16.2 %collective-permute-start.6 = (bf16[1,16,16,768]{3,2,1,0:T(8,128)(2,1)}, bf16[1,16,16,768]{3,2,1,0:T(8,128)(2,1)}, u32[]{:S(2)}, u32[]{:S(2)}) collective-permute-start(bf16[1,16,16,768]{3,2,1,0:T(8,128)(2,1)} %copy-done.2), channel_id=1, source_target_pairs={{0,16},{16,32},{32,48},{48,64},{64,80},{80,96},{96,112},{112,128},... | collective-permute-start | bytes 1179656 | tf_op jit(solution)/shard_map/ppermute | solution.py:12
  140.9 4.2 %copy-start.4 = (bf16[1024,768]{0,1:T(8,128)(2,1)S(1)}, bf16[1024,768]{0,1:T(8,128)(2,1)}, u32[]{:S(2)}) copy-start(bf16[1024,768]{0,1:T(8,128)(2,1)} %copy.54) | copy-start | bytes 4718596
  140.9 4.2 %copy-start.8 = (s32[1024]{0:T(1024)S(1)}, s32[1024]{0:T(1024)}, u32[]{:S(2)}) copy-start(s32[1024]{0:T(1024)} %add_select_fusion) | copy-start | bytes 12292
where the time goes:
time: 160 us; the launch traced here: 158 us
  starting transfers between devices  48.2 us (30%)
  blocking collectives  39.2 us (25%)
  matrix products  25.8 us (16%)
  waiting for transfers between devices  21.5 us (13%)
  local copies, waits for them, and re-layouts  18.8 us (12%)
  other arithmetic  3.18 us (2%)
    all_to_all x2, blocking collectives, ham(): lax.all_to_all(packed, 'rad', split_axis=2, concat_axis=1, tiled=True)  27.4 us
    ppermute x7, starting transfers between devices, from_behind(): return lax.ppermute(block, axis, route)  25.4 us
    all_to_all x3, starting transfers between devices, ham(): lax.all_to_all(kin_moved, 'rad', split_axis=1, concat_axis=2, tiled=True)  17 us
    ppermute x7, waiting for transfers between devices, from_behind(): return lax.ppermute(block, axis, route)  14.4 us
    all_to_all x1, blocking collectives, sent_and_summed(): lax.all_to_all(tiles, axis, split_axis=0, concat_axis=0, tiled=True)  11.8 us
    dot_general x3, matrix products, ham(): lax.dot_general(scaled.reshape(-1, nquad), basis, (((1,), (1,)), ((), ())...  11 us
    dot_general x3, matrix products, ham(): jnp.dot(packed.reshape(-1, nang), basis, preferred_element_type=jnp.float32)  9.47 us
    transpose x3, local copies, waits for them, and re-layouts, ham(): jnp.einsum('rs,ksvj->krvj', kinetic, regrouped, preferred_element_type=jn...  9.15 us
  transfers between devices with their start and end apart: 11, of which 7 were waited for; matrix products, arithmetic and copies ran while one was open for 14% of the time, Pallas kernels for 0%

commit v1 on v0

v1 whole, which is shorter than its diff:
```python
import jax
import jax.numpy as jnp
from jax import lax
from jax.sharding import PartitionSpec as P

ITERS = 3


def from_behind(block, axis, distance):
    devices = range(lax.axis_size(axis))
    route = [(i - distance, i) for i in devices if i - distance in devices]
    return lax.ppermute(block, axis, route)


def per_device(
    psi_start,
    potential,
    basis,
    kinetic,
    radial_factor,
    damping,
    coupling,
    helicity,
    chan_rad,
    chan_vib,
    projector,
):
    _, rdev, nvib, nang = psi_start.shape
    nquad = basis.shape[1]
    rad_index = lax.axis_index("rad")
    hel_index = lax.axis_index("hel")
    last = lax.axis_size("hel") - 1
    coupling_eff = jnp.where(hel_index < last, coupling, jnp.zeros_like(coupling))
    coupling_prev = from_behind(coupling_eff, "hel", 1).astype(jnp.float32)
    coupling_eff = coupling_eff.astype(jnp.float32)
    kvalue = helicity.astype(jnp.float32)[0]
    scales = lax.all_gather(jnp.stack([radial_factor, damping]), "rad", axis=1, tiled=True)
    cen_factor = (-2.0 * kvalue * kvalue * scales[0])[:, None]
    damp = scales[1][:, None]
    psi = lax.all_to_all(
        psi_start[0].astype(jnp.bfloat16), "rad", split_axis=1, concat_axis=0, tiled=True
    ).reshape(-1, nang)
    pot = lax.all_to_all(
        potential.astype(jnp.bfloat16), "rad", split_axis=1, concat_axis=0, tiled=True
    ).reshape(-1, nquad)

    def ham(psi):
        packed = psi.astype(jnp.bfloat16)
        lower = from_behind(packed, "hel", 1).astype(jnp.float32)
        upper = from_behind(packed, "hel", -1).astype(jnp.float32)
        kin = jnp.dot(kinetic, packed, preferred_element_type=jnp.float32)
        grid = jnp.dot(packed, basis, preferred_element_type=jnp.float32)
        scaled = (grid * pot).astype(jnp.bfloat16)
        ang = lax.dot_general(
            scaled, basis, (((1,), (1,)), ((), ())), preferred_element_type=jnp.float32
        )
        cor = coupling_eff * upper + coupling_prev * lower
        return kin + ang + cen_factor * psi + cor

    previous = psi.astype(jnp.float32)
    current = damp * ham(previous)
    for step in range(ITERS - 1):
        following = damp * (2.0 * ham(current) - damp * previous)
        previous, current = (current, following)
    final_b = current.astype(jnp.bfloat16)
    back = lax.all_to_all(
        final_b.reshape(-1, 1, nang), "rad", split_axis=0, concat_axis=1, tiled=True
    )
    psi_final = back.astype(jnp.float32)[None]
    hits = lax.dot_general(
        projector, final_b, (((1,), (1,)), ((), ())), preferred_element_type=jnp.float32
    )
    slot = jnp.where(chan_vib == rad_index, chan_rad, -1)
    chosen = slot[:, None] == jnp.arange(final_b.shape[0], dtype=jnp.int32)[None, :]
    partial_amp = jnp.sum(jnp.where(chosen, hits, 0.0), axis=1)
    tiles = partial_amp.reshape(lax.axis_size("rad"), -1)
    arrived = lax.all_to_all(tiles, "rad", split_axis=0, concat_axis=0, tiled=True)
    amplitude = arrived.sum(axis=0)[None]
    return (psi_final, amplitude)


def solution(mesh):
    placed = (
        P("hel", "rad", None, None),
        P("rad", None, None),
        P(),
        P(),
        P("rad"),
        P("rad"),
        P("hel", None),
        P("hel"),
        P(),
        P(),
        P(),
    )
    return jax.shard_map(
        per_device,
        mesh=mesh,
        in_specs=placed,
        out_specs=(P("hel", "rad", None, None), P("hel", "rad")),
        check_vma=False,
    )
```

time: 160 us -> 139 us (0.87)
  the two profiles are of different devices: /device:TPU:5 before, /device:TPU:4 now
where the time goes in v1:
time: 139 us; the launch traced here: 138 us
  starting transfers between devices  41.8 us (30%)
  waiting for transfers between devices  39.4 us (28%)
  blocking collectives  19.9 us (14%)
  matrix products  19.9 us (14%)
  local copies, waits for them, and re-layouts  9.43 us (7%)
  other arithmetic  6.04 us (4%)
  between operations  1.46 us (1%)
    ppermute x7, waiting for transfers between devices, from_behind(): return lax.ppermute(block, axis, route)  24.4 us
    ppermute x7, starting transfers between devices, from_behind(): return lax.ppermute(block, axis, route)  23.5 us
    all_gather x1, blocking collectives, per_device(): lax.all_gather(jnp.stack([radial_factor, damping]), 'rad', axis=1, tiled=...  19.9 us
    dot_general x3, matrix products, ham(): lax.dot_general(scaled, basis, (((1,), (1,)), ((), ())), preferred_elemen...  12 us
    all_to_all x1, waiting for transfers between devices, per_device(): lax.all_to_all(final_b.reshape(-1, 1, nang), 'rad', split_axis=0, concat_...  8.89 us
    dot_general x3, matrix products, ham(): kin = jnp.dot(kinetic, packed, preferred_element_type=jnp.float32)  7.32 us
    unnamed x17, local copies, waits for them, and re-layouts  6.9 us
    all_to_all x1, starting transfers between devices, per_device(): lax.all_to_all(tiles, 'rad', split_axis=0, concat_axis=0, tiled=True)  5.82 us
  transfers between devices with their start and end apart: 11, of which 9 were waited for; matrix products, arithmetic and copies ran while one was open for 15% of the time, Pallas kernels for 0%

profile of v1, /device:TPU:4, one launch (start us, length us, event | category | flops | bytes accessed | tf_op | source)
XLA Modules:
  0.0 138.0 jit_solution(12392743322029272148)
XLA Ops:
  0.6 0.0 copy-start
  0.6 2.5 %copy.54 = bf16[1,16,16,768]{3,1,2,0:T(8,128)(2,1)} copy(f32[1,16,16,768]{3,2,1,0:T(8,128)} %param.11) | data formatting | bytes 1179648 | tf_op args[0]
  3.1 5.3 %all-to-all-start = ((bf16[16,16,768]{2,0,1:T(8,128)(2,1)}), bf16[16,16,768]{2,0,1:T(8,128)(2,1)S(1)}, u32[]{:S(2)}, u32[]{:S(2)}) async-start(bf16[16,16,768]{2,0,1:T(8,128)(2,1)} %bitcast.74), calls=%async_computation | async-start | bytes 786432 | tf_op jit(solution)/shard_map/all_to_all | solution.py:40
  8.5 1.3 convert_reduce_fusion.1
  9.7 3.8 %collective-permute-start.1 = (bf16[1,768]{1,0:T(2,128)(2,1)}, bf16[1,768]{1,0:T(2,128)(2,1)}, u32[]{:S(2)}, u32[]{:S(2)}) collective-permute-start(bf16[1,768]{1,0:T(2,128)(2,1)} %get-tuple-element.3), channel_id=1, source_target_pairs={{0,16},{16,32},{32,48},{48,64},{64,80},{80,96},{96,112},{112,128},... | collective-permute-start | bytes 4616 | tf_op jit(solution)/shard_map/ppermute | solution.py:12
  14.2 0.7 maximum_bitcast_fusion
  14.9 19.9 %all-gather = f32[16,16,2]{1,2,0:T(2,128)S(1)} all-gather(f32[1,16,2]{1,2,0:T(2,128)S(1)} %maximum_bitcast_fusion), channel_id=1, replica_groups=mesh['hel'=16,'rad'=16] {'rad'}, dimensions={0}, use_global_device_ids=true | all-gather | bytes 2176 | tf_op jit(solution)/shard_map/all_gather | solution.py:37
  34.8 0.1 reshape.54
  34.9 3.1 %copy.52 = bf16[16,16,1536]{2,0,1:T(8,128)(2,1)} copy(f32[16,16,1536]{2,1,0:T(8,128)} %param.12) | data formatting | bytes 2359296 | tf_op args[1]
  38.0 0.0 all-to-all-done
  38.0 3.6 %all-to-all-start.1 = ((bf16[16,16,1536]{2,0,1:T(8,128)(2,1)}), bf16[16,16,1536]{2,0,1:T(8,128)(2,1)S(1)}, u32[]{:S(2)}, u32[]{:S(2)}) async-start(bf16[16,16,1536]{2,0,1:T(8,128)(2,1)} %copy.52), calls=%async_computation.1 | async-start | bytes 1572864 | tf_op jit(solution)/shard_map/all_to_all | solution.py:43
  41.7 0.0 copy-done.2
  41.7 0.0 copy-done.3
  41.7 0.6 compare_select_fusion
  42.3 0.0 collective-permute-done.1
  42.3 0.7 convert_reduce_fusion
  43.0 6.1 %collective-permute-start = (bf16[256,768]{1,0:T(8,128)(2,1)S(1)}, bf16[256,768]{1,0:T(8,128)(2,1)}, u32[]{:S(2)}, u32[]{:S(2)}) collective-permute-start(bf16[256,768]{1,0:T(8,128)(2,1)S(1)} %bitcast.75), channel_id=1, source_target_pairs={{16,0},{32,16},{48,32},{64,48},{80,64},{96,80},{112,96},{128,112},... | collective-permute-start | bytes 1179656 | tf_op jit(solution)/shard_map/ppermute | solution.py:12
  49.1 1.9 %collective-permute-start.2 = (bf16[256,768]{1,0:T(8,128)(2,1)S(1)}, bf16[256,768]{1,0:T(8,128)(2,1)}, u32[]{:S(2)}, u32[]{:S(2)}) collective-permute-start(bf16[256,768]{1,0:T(8,128)(2,1)S(1)} %bitcast.76), channel_id=1, source_target_pairs={{0,16},{16,32},{32,48},{48,64},{64,80},{80,96},{96,112},{112,128},... | collective-permute-start | bytes 1179656 | tf_op jit(solution)/shard_map/ppermute | solution.py:12
  51.0 2.1 %fusion.18 = f32[256,768]{1,0:T(8,128)} fusion(bf16[256,256]{1,0:T(8,128)(2,1)} %param.14, bf16[256,768]{1,0:T(8,128)(2,1)S(1)} %bitcast.77), kind=kOutput, calls=%fused_computation.40 | convolution fusion | flops 100663296 | bytes 1310720 | tf_op jit(solution)/shard_map/dot_general | solution.py:51
  53.1 2.3 %all-to-all-done.1 = bf16[16,16,1536]{2,0,1:T(8,128)(2,1)S(1)} async-done(((bf16[16,16,1536]{2,0,1:T(8,128)(2,1)}), bf16[16,16,1536]{2,0,1:T(8,128)(2,1)S(1)}, u32[]{:S(2)}, u32[]{:S(2)}) %all-to-all-start.1) | async-done | bytes 786464 | tf_op jit(solution)/shard_map/all_to_all | solution.py:43
  55.4 1.3 bitcast_convert_fusion
  56.7 1.2 collective-permute-done
  57.9 7.8 %collective-permute-done.2 = bf16[256,768]{1,0:T(8,128)(2,1)} collective-permute-done((bf16[256,768]{1,0:T(8,128)(2,1)S(1)}, bf16[256,768]{1,0:T(8,128)(2,1)}, u32[]{:S(2)}, u32[]{:S(2)}) %collective-permute-start.2) | collective-permute-done | bytes 393248 | tf_op jit(solution)/shard_map/ppermute | solution.py:12
  65.7 4.1 %fusion.16 = (bf16[256,768]{1,0:T(8,128)(2,1)}, f32[256,768]{1,0:T(8,128)S(1)}) fusion(bf16[256,768]{1,0:T(8,128)(2,1)} %collective-permute-done.2, f32[768]{0:T(1024)S(1)} %convert_reduce_fusion, bf16[256,768]{1,0:T(8,128)(2,1)} %collective-permute-done, f32[768]{0:T(1024)S(1)} %get-tuple-element.2, bf16[256,768]{1,0:T(8,128)(2,1)S(1)} %bitcast.78, ...), kind=kOutput, calls=%fused_computation.38 | convolution fusion | flops 1211105280 | bytes 7086080 | tf_op jit(solution)/shard_map/dot_general | solution.py:54
  69.9 1.9 %collective-permute-start.3 = (bf16[256,768]{1,0:T(8,128)(2,1)}, bf16[256,768]{1,0:T(8,128)(2,1)}, u32[]{:S(2)}, u32[]{:S(2)}) collective-permute-start(bf16[256,768]{1,0:T(8,128)(2,1)} %get-tuple-element.6), channel_id=1, source_target_pairs={{16,0},{32,16},{48,32},{64,48},{80,64},{96,80},{112,96},{128,112},... | collective-permute-start | bytes 1179656 | tf_op jit(solution)/shard_map/ppermute | solution.py:12
  71.8 3.9 %collective-permute-start.4 = (bf16[256,768]{1,0:T(8,128)(2,1)}, bf16[256,768]{1,0:T(8,128)(2,1)}, u32[]{:S(2)}, u32[]{:S(2)}) collective-permute-start(bf16[256,768]{1,0:T(8,128)(2,1)} %get-tuple-element.6), channel_id=1, source_target_pairs={{0,16},{16,32},{32,48},{48,64},{64,80},{80,96},{96,112},{112,128},... | collective-permute-start | bytes 1179656 | tf_op jit(solution)/shard_map/ppermute | solution.py:12
  75.7 3.9 %fusion.11 = f32[256,768]{1,0:T(8,128)} fusion(bf16[768,1536]{1,0:T(8,128)(2,1)S(1)} %copy-done, f32[256,1536]{1,0:T(8,128)} %bitcast.81, bf16[256,768]{1,0:T(8,128)(2,1)} %get-tuple-element.6), kind=kOutput, calls=%fused_computation.22 | convolution fusion | flops 1208745984 | bytes 5111808 | tf_op jit(solution)/shard_map/dot_general | solution.py:54
  79.6 2.6 %collective-permute-done.3 = bf16[256,768]{1,0:T(8,128)(2,1)} collective-permute-done((bf16[256,768]{1,0:T(8,128)(2,1)}, bf16[256,768]{1,0:T(8,128)(2,1)}, u32[]{:S(2)}, u32[]{:S(2)}) %collective-permute-start.3) | collective-permute-done | bytes 393248 | tf_op jit(solution)/shard_map/ppermute | solution.py:12
  82.2 5.5 %collective-permute-done.4 = bf16[256,768]{1,0:T(8,128)(2,1)} collective-permute-done((bf16[256,768]{1,0:T(8,128)(2,1)}, bf16[256,768]{1,0:T(8,128)(2,1)}, u32[]{:S(2)}, u32[]{:S(2)}) %collective-permute-start.4) | collective-permute-done | bytes 393248 | tf_op jit(solution)/shard_map/ppermute | solution.py:12
  87.8 3.0 %fusion.17 = (bf16[256,768]{1,0:T(8,128)(2,1)}, f32[256,768]{1,0:T(8,128)}) fusion(bf16[256,768]{1,0:T(8,128)(2,1)S(1)} %bitcast.79, bf16[256,768]{1,0:T(8,128)(2,1)} %collective-permute-done.4, f32[768]{0:T(1024)S(1)} %convert_reduce_fusion, bf16[256,768]{1,0:T(8,128)(2,1)} %collective-permute-done.3, f32[768]{0:T(1024)S(1)} %get-tuple-element.2, ...), kind=kOutput, calls=%fused_computation.39 | convolution fusion | flops 103612416 | bytes 4464640 | tf_op jit(solution)/shard_map/dot_general | solution.py:51
  90.8 1.9 %collective-permute-start.5 = (bf16[256,768]{1,0:T(8,128)(2,1)}, bf16[256,768]{1,0:T(8,128)(2,1)S(1)}, u32[]{:S(2)}, u32[]{:S(2)}) collective-permute-start(bf16[256,768]{1,0:T(8,128)(2,1)} %get-tuple-element.8), channel_id=1, source_target_pairs={{16,0},{32,16},{48,32},{64,48},{80,64},{96,80},{112,96},{128,112},... | collective-permute-start | bytes 1179656 | tf_op jit(solution)/shard_map/ppermute | solution.py:12
  92.7 3.9 %collective-permute-start.6 = (bf16[256,768]{1,0:T(8,128)(2,1)}, bf16[256,768]{1,0:T(8,128)(2,1)}, u32[]{:S(2)}, u32[]{:S(2)}) collective-permute-start(bf16[256,768]{1,0:T(8,128)(2,1)} %get-tuple-element.8), channel_id=1, source_target_pairs={{0,16},{16,32},{32,48},{48,64},{64,80},{80,96},{96,112},{112,128},... | collective-permute-start | bytes 1179656 | tf_op jit(solution)/shard_map/ppermute | solution.py:12
  96.7 3.9 %fusion.10 = f32[256,768]{1,0:T(8,128)} fusion(bf16[768,1536]{1,0:T(8,128)(2,1)S(1)} %copy-done, f32[256,1536]{1,0:T(8,128)} %bitcast.82, bf16[256,768]{1,0:T(8,128)(2,1)} %get-tuple-element.8), kind=kOutput, calls=%fused_computation.21 | convolution fusion | flops 1208745984 | bytes 5111808 | tf_op jit(solution)/shard_map/dot_general | solution.py:54
  100.6 1.6 %collective-permute-done.5 = bf16[256,768]{1,0:T(8,128)(2,1)S(1)} collective-permute-done((bf16[256,768]{1,0:T(8,128)(2,1)}, bf16[256,768]{1,0:T(8,128)(2,1)S(1)}, u32[]{:S(2)}, u32[]{:S(2)}) %collective-permute-start.5) | collective-permute-done | bytes 393248 | tf_op jit(solution)/shard_map/ppermute | solution.py:12
  102.2 5.7 %collective-permute-done.6 = bf16[256,768]{1,0:T(8,128)(2,1)} collective-permute-done((bf16[256,768]{1,0:T(8,128)(2,1)}, bf16[256,768]{1,0:T(8,128)(2,1)}, u32[]{:S(2)}, u32[]{:S(2)}) %collective-permute-start.6) | collective-permute-done | bytes 393248 | tf_op jit(solution)/shard_map/ppermute | solution.py:12
  107.9 2.2 %multiply_convert_fusion = bf16[256,768]{1,0:T(8,128)(2,1)S(1)} fusion(f32[256,768]{1,0:T(8,128)S(1)} %get-tuple-element.7, bf16[256,768]{1,0:T(8,128)(2,1)} %collective-permute-done.6, bf16[256,768]{1,0:T(8,128)(2,1)} %copy-done.1, f32[256,768]{1,0:T(8,128)} %get-tuple-element.9, f32[256,768]{1,0:T(8,128)} %fusion.10, bf16[256,256]{1,0:T(8,128)(2,1)} %param.14, ...), kind=kOutput, calls=%fused_computation.28 | convolution fusion | flops 103415808 | bytes 4071424 | tf_op jit(solution)/shard_map/dot_general | solution.py:51
  110.2 0.6 fusion.9
  110.8 0.7 all_to_all.36
  111.4 5.8 %all-to-all-start.3 = ((f32[16,1,64]{2,1,0:T(1,128)}), f32[16,1,64]{2,1,0:T(1,128)S(1)}, u32[]{:S(2)}, u32[]{:S(2)}) async-start(f32[16,1,64]{2,1,0:T(1,128)} %all_to_all.36), calls=%async_computation.3 | async-start | bytes 16384 | tf_op jit(solution)/shard_map/all_to_all | solution.py:77
  117.3 0.5 broadcast.15
  117.8 0.9 reduce.5
  118.7 0.8 reshape.57
  119.6 3.8 %all-to-all-done.3 = f32[16,1,64]{2,1,0:T(1,128)S(1)} async-done(((f32[16,1,64]{2,1,0:T(1,128)}), f32[16,1,64]{2,1,0:T(1,128)S(1)}, u32[]{:S(2)}, u32[]{:S(2)}) %all-to-all-start.3) | async-done | bytes 4128 | tf_op jit(solution)/shard_map/all_to_all | solution.py:77
  123.3 3.6 %all-to-all-start.2 = ((bf16[16,2,6144]{2,1,0:T(2,128)(2,1)}), bf16[16,2,6144]{2,1,0:T(2,128)(2,1)S(1)}, u32[]{:S(2)}, u32[]{:S(2)}) async-start(bf16[16,2,6144]{2,1,0:T(2,128)(2,1)} %reshape.57), calls=%async_computation.2 | async-start | bytes 786432 | tf_op jit(solution)/shard_map/all_to_all | solution.py:66
  126.9 0.5 reduce_sum.19
  127.4 8.9 %all-to-all-done.2 = bf16[16,2,6144]{2,1,0:T(2,128)(2,1)S(1)} async-done(((bf16[16,2,6144]{2,1,0:T(2,128)(2,1)}), bf16[16,2,6144]{2,1,0:T(2,128)(2,1)S(1)}, u32[]{:S(2)}, u32[]{:S(2)}) %all-to-all-start.2) | async-done | bytes 393248 | tf_op jit(solution)/shard_map/all_to_all | solution.py:66
  136.3 0.4 reshape.58
  136.7 1.3 copy.53
  (11 shorter events, 0.0 us)
Async XLA Ops:
  0.6 65.1 %copy-start = (bf16[768,1536]{1,0:T(8,128)(2,1)S(1)}, bf16[768,1536]{1,0:T(8,128)(2,1)}, u32[]{:S(2)}) copy-start(bf16[768,1536]{1,0:T(8,128)(2,1)} %param.13) | copy-start | bytes 7077892
  3.1 38.6 %copy-start.2 = (s32[1024]{0:T(1024)S(1)}, s32[1024]{0:T(1024)}, u32[]{:S(2)}) copy-start(s32[1024]{0:T(1024)} %param.19) | copy-start | bytes 12292
  3.1 38.6 %copy-start.3 = (s32[1024]{0:T(1024)S(1)}, s32[1024]{0:T(1024)}, u32[]{:S(2)}) copy-start(s32[1024]{0:T(1024)} %param.20) | copy-start | bytes 12292
  3.1 34.9 %all-to-all-start = ((bf16[16,16,768]{2,0,1:T(8,128)(2,1)}), bf16[16,16,768]{2,0,1:T(8,128)(2,1)S(1)}, u32[]{:S(2)}, u32[]{:S(2)}) async-start(bf16[16,16,768]{2,0,1:T(8,128)(2,1)} %bitcast.74), calls=%async_computation | async-start | bytes 786432 | tf_op jit(solution)/shard_map/all_to_all | solution.py:40
  9.7 32.6 %collective-permute-start.1 = (bf16[1,768]{1,0:T(2,128)(2,1)}, bf16[1,768]{1,0:T(2,128)(2,1)}, u32[]{:S(2)}, u32[]{:S(2)}) collective-permute-start(bf16[1,768]{1,0:T(2,128)(2,1)} %get-tuple-element.3), channel_id=1, source_target_pairs={{0,16},{16,32},{32,48},{48,64},{64,80},{80,96},{96,112},{112,128},... | collective-permute-start | bytes 4616 | tf_op jit(solution)/shard_map/ppermute | solution.py:12
  38.0 17.3 %all-to-all-start.1 = ((bf16[16,16,1536]{2,0,1:T(8,128)(2,1)}), bf16[16,16,1536]{2,0,1:T(8,128)(2,1)S(1)}, u32[]{:S(2)}, u32[]{:S(2)}) async-start(bf16[16,16,1536]{2,0,1:T(8,128)(2,1)} %copy.52), calls=%async_computation.1 | async-start | bytes 1572864 | tf_op jit(solution)/shard_map/all_to_all | solution.py:43
  43.0 14.9 %collective-permute-start = (bf16[256,768]{1,0:T(8,128)(2,1)S(1)}, bf16[256,768]{1,0:T(8,128)(2,1)}, u32[]{:S(2)}, u32[]{:S(2)}) collective-permute-start(bf16[256,768]{1,0:T(8,128)(2,1)S(1)} %bitcast.75), channel_id=1, source_target_pairs={{16,0},{32,16},{48,32},{64,48},{80,64},{96,80},{112,96},{128,112},... | collective-permute-start | bytes 1179656 | tf_op jit(solution)/shard_map/ppermute | solution.py:12
  49.1 16.6 %collective-permute-start.2 = (bf16[256,768]{1,0:T(8,128)(2,1)S(1)}, bf16[256,768]{1,0:T(8,128)(2,1)}, u32[]{:S(2)}, u32[]{:S(2)}) collective-permute-start(bf16[256,768]{1,0:T(8,128)(2,1)S(1)} %bitcast.76), channel_id=1, source_target_pairs={{0,16},{16,32},{32,48},{48,64},{64,80},{80,96},{96,112},{112,128},... | collective-permute-start | bytes 1179656 | tf_op jit(solution)/shard_map/ppermute | solution.py:12
  69.9 12.4 %collective-permute-start.3 = (bf16[256,768]{1,0:T(8,128)(2,1)}, bf16[256,768]{1,0:T(8,128)(2,1)}, u32[]{:S(2)}, u32[]{:S(2)}) collective-permute-start(bf16[256,768]{1,0:T(8,128)(2,1)} %get-tuple-element.6), channel_id=1, source_target_pairs={{16,0},{32,16},{48,32},{64,48},{80,64},{96,80},{112,96},{128,112},... | collective-permute-start | bytes 1179656 | tf_op jit(solution)/shard_map/ppermute | solution.py:12
  71.8 16.0 %collective-permute-start.4 = (bf16[256,768]{1,0:T(8,128)(2,1)}, bf16[256,768]{1,0:T(8,128)(2,1)}, u32[]{:S(2)}, u32[]{:S(2)}) collective-permute-start(bf16[256,768]{1,0:T(8,128)(2,1)} %get-tuple-element.6), channel_id=1, source_target_pairs={{0,16},{16,32},{32,48},{48,64},{64,80},{80,96},{96,112},{112,128},... | collective-permute-start | bytes 1179656 | tf_op jit(solution)/shard_map/ppermute | solution.py:12
  90.8 11.3 %collective-permute-start.5 = (bf16[256,768]{1,0:T(8,128)(2,1)}, bf16[256,768]{1,0:T(8,128)(2,1)S(1)}, u32[]{:S(2)}, u32[]{:S(2)}) collective-permute-start(bf16[256,768]{1,0:T(8,128)(2,1)} %get-tuple-element.8), channel_id=1, source_target_pairs={{16,0},{32,16},{48,32},{64,48},{80,64},{96,80},{112,96},{128,112},... | collective-permute-start | bytes 1179656 | tf_op jit(solution)/shard_map/ppermute | solution.py:12
  92.7 15.2 %collective-permute-start.6 = (bf16[256,768]{1,0:T(8,128)(2,1)}, bf16[256,768]{1,0:T(8,128)(2,1)}, u32[]{:S(2)}, u32[]{:S(2)}) collective-permute-start(bf16[256,768]{1,0:T(8,128)(2,1)} %get-tuple-element.8), channel_id=1, source_target_pairs={{0,16},{16,32},{32,48},{48,64},{64,80},{80,96},{96,112},{112,128},... | collective-permute-start | bytes 1179656 | tf_op jit(solution)/shard_map/ppermute | solution.py:12
  100.6 9.6 %copy-start.4 = (s32[1024]{0:T(1024)S(1)}, s32[1024]{0:T(1024)}, u32[]{:S(2)}) copy-start(s32[1024]{0:T(1024)} %compare_select_fusion) | copy-start | bytes 12292
  100.6 9.6 %copy-start.5 = (bf16[1024,768]{1,0:T(8,128)(2,1)S(1)}, bf16[1024,768]{1,0:T(8,128)(2,1)}, u32[]{:S(2)}) copy-start(bf16[1024,768]{1,0:T(8,128)(2,1)} %param.21) | copy-start | bytes 4718596
  102.2 5.7 %copy-start.1 = (bf16[256,768]{1,0:T(8,128)(2,1)}, bf16[256,768]{1,0:T(8,128)(2,1)S(1)}, u32[]{:S(2)}) copy-start(bf16[256,768]{1,0:T(8,128)(2,1)S(1)} %collective-permute-done.5) | copy-start | bytes 1179652
  111.4 11.9 %all-to-all-start.3 = ((f32[16,1,64]{2,1,0:T(1,128)}), f32[16,1,64]{2,1,0:T(1,128)S(1)}, u32[]{:S(2)}, u32[]{:S(2)}) async-start(f32[16,1,64]{2,1,0:T(1,128)} %all_to_all.36), calls=%async_computation.3 | async-start | bytes 16384 | tf_op jit(solution)/shard_map/all_to_all | solution.py:77
  123.3 13.0 %all-to-all-start.2 = ((bf16[16,2,6144]{2,1,0:T(2,128)(2,1)}), bf16[16,2,6144]{2,1,0:T(2,128)(2,1)S(1)}, u32[]{:S(2)}, u32[]{:S(2)}) async-start(bf16[16,2,6144]{2,1,0:T(2,128)(2,1)} %reshape.57), calls=%async_computation.2 | async-start | bytes 786432 | tf_op jit(solution)/shard_map/all_to_all | solution.py:66

commit v2 on v1

v2 whole, which is shorter than its diff:
```python
import jax
import jax.numpy as jnp
from jax import lax
from jax.experimental import pallas as pl
from jax.experimental.pallas import tpu as pltpu
from jax.sharding import PartitionSpec as P

ITERS = 3
MESH = pl.DeviceIdType.MESH
F32 = jnp.float32
BF16 = jnp.bfloat16
NCH = 16
ZS = 8
LANES = 128


def kernel(
    psi_hbm,
    pot_hbm,
    basis_hbm,
    kin_hbm,
    proj_hbm,
    rf_s,
    damp_s,
    hel_s,
    coup_ref,
    crad_ref,
    cvib_ref,
    fin_ref,
    amp_ref,
    psi_v,
    pot_v,
    basis,
    kin,
    proj,
    stage,
    pstage,
    tile,
    tiles,
    ce,
    cp,
    pb,
    lo,
    up,
    fw,
    pot,
    scaled,
    tot,
    dmp,
    cen,
    asend,
    arecv,
    load_sem,
    psi_l,
    pot_l,
    psi_s,
    psi_r,
    til_s,
    til_r,
    pot_s,
    pot_r,
    sib_s,
    sib_r,
    lo_s,
    lo_r,
    up_s,
    up_r,
    cp_s,
    cp_r,
    fin_s,
    fin_r,
    amp_s,
    amp_r,
):
    hel, rad = lax.axis_index("hel"), lax.axis_index("rad")
    x_hi, z = hel // ZS, hel % ZS
    x_lo, y, core = rad // 8, (rad // 2) % 4, rad % 2
    v_me = x_hi * 8 + x_lo * 4 + y
    k_me = core * ZS + z
    above = (x_hi * ZS + (z + 1) % ZS, x_lo * 8 + y * 2 + (core + (z + 1) // ZS) % 2)
    below = (
        x_hi * ZS + (z + ZS - 1) % ZS,
        x_lo * 8 + y * 2 + (core + 1 - (z + ZS - 1) // ZS) % 2,
    )
    sibling = (hel, x_lo * 8 + y * 2 + 1 - core)
    rows, nang = pb.shape[1:]
    nquad = pot.shape[1]
    part = rows // NCH

    def load_lanes(b, carry):
        cols = pl.ds(pl.multiple_of(b * LANES, LANES), LANES)
        pltpu.make_async_copy(psi_hbm.at[:, cols], psi_v.at[b], psi_l.at[b]).start()
        return carry

    def load_pot_lanes(b, carry):
        cols = pl.ds(pl.multiple_of(b * LANES, LANES), LANES)
        pltpu.make_async_copy(pot_hbm.at[:, cols], pot_v.at[b], pot_l.at[b]).start()
        return carry

    lax.fori_loop(0, nang // LANES, load_lanes, 0)
    lax.fori_loop(0, nquad // LANES, load_pot_lanes, 0)
    loads = [
        pltpu.make_async_copy(src, dst, load_sem.at[i])
        for i, (src, dst) in enumerate([(kin_hbm, kin), (basis_hbm, basis), (proj_hbm, proj)])
    ]
    for load in loads:
        load.start()

    barrier = pltpu.get_barrier_semaphore()
    here = x_hi * NCH + rad

    def greet(i, carry):
        other = (here + 1 + i) % (2 * NCH)
        pl.semaphore_signal(
            barrier,
            inc=1,
            device_id=((other // NCH) * ZS + z, other % NCH),
            device_id_type=MESH,
        )
        return carry

    lax.fori_loop(0, 2 * NCH - 1, greet, 0)
    for neighbour in (above, below):
        pl.semaphore_signal(barrier, inc=1, device_id=neighbour, device_id_type=MESH)

    def chunk(i):
        return pl.ds(pl.multiple_of(i * part, part), part)

    def remote(src, dst, send, recv, device):
        return pltpu.make_async_remote_copy(
            src_ref=src,
            dst_ref=dst,
            send_sem=send,
            recv_sem=recv,
            device_id=device,
            device_id_type=MESH,
        )

    def is_here(device):
        return (device[0] == hel) & (device[1] == rad)

    def push(src, dst, send, recv, device):
        mine = is_here(device)

        @pl.when(mine)
        def _():
            pltpu.make_async_copy(src, dst, recv).start()

        @pl.when(jnp.logical_not(mine))
        def _():
            remote(src, dst, send, recv, device).start()

    def pushed(src, dst, send, recv, device):
        @pl.when(jnp.logical_not(is_here(device)))
        def _():
            remote(src, dst, send, recv, device).wait_send()

    sub = lax.broadcasted_iota(jnp.int32, (8, LANES), 0)
    lane = lax.broadcasted_iota(jnp.int32, (8, LANES), 1)
    kvalue = hel_s[0].astype(F32)
    small = jnp.zeros((8, LANES), F32)
    for i in range(part):
        small = jnp.where((sub == 0) & (lane == i), damp_s[i], small)
        small = jnp.where(
            (sub == 0) & (lane == part + i), -2.0 * (kvalue * kvalue) * rf_s[i], small
        )
    tile[...] = small
    wide = coup_ref[...].astype(F32)
    for b in range(nang // LANES):
        tile[2 + b : 3 + b, :] = wide[:, b * LANES : (b + 1) * LANES]

    for b in range(nang // LANES):
        cols = slice(b * LANES, (b + 1) * LANES)
        pltpu.make_async_copy(psi_hbm.at[:, cols], psi_v.at[b], psi_l.at[b]).wait()
        for v in range(NCH):
            stage[v, :, cols] = psi_v[b, pl.ds(v, part, stride=NCH), :].astype(BF16)
    pl.semaphore_wait(barrier, 2 * NCH + 1)

    def holder(s):
        v = (rad + s) % NCH
        return v, ((v // 8) * ZS + z, v % 8 * 2 + x_hi)

    def send_psi(s, carry):
        v, device = holder(s)
        push(stage.at[v], pb.at[0, chunk(rad), :], psi_s.at[s], psi_r.at[rad], device)
        return carry

    def send_tile(s, carry):
        v, device = holder(s)
        push(tile, tiles.at[rad], til_s.at[s], til_r.at[rad], device)
        return carry

    lax.fori_loop(0, NCH, send_psi, 0)
    lax.fori_loop(0, NCH, send_tile, 0)

    for b in range(nquad // LANES):
        cols = slice(b * LANES, (b + 1) * LANES)
        pltpu.make_async_copy(pot_hbm.at[:, cols], pot_v.at[b], pot_l.at[b]).wait()
        for i in range(NCH // 2):
            pstage[i, :, cols] = pot_v[b, pl.ds(x_hi * 8 + i, part, stride=NCH), :].astype(BF16)

    def pot_holder(s):
        i = (rad // 2 + s) % 8
        return i, (hel, 2 * i + core)

    def send_pot(s, carry):
        i, device = pot_holder(s)
        push(pstage.at[i], pot.at[chunk(rad), :], pot_s.at[s], pot_r.at[rad // 2], device)
        return carry

    lax.fori_loop(0, NCH // 2, send_pot, 0)

    def send_on(n, i):
        remote(
            pb.at[n, chunk(i), :], lo.at[n, chunk(i), :], lo_s.at[n, i], lo_r.at[n, i], above
        ).start()
        remote(
            pb.at[n, chunk(i), :], up.at[n, chunk(i), :], up_s.at[n, i], up_r.at[n, i], below
        ).start()

    def order(s):
        return (v_me + NCH - s) % NCH

    def take_psi(s, carry):
        i = order(s)
        pltpu.make_async_copy(stage.at[0], pb.at[0, chunk(i), :], psi_r.at[i]).wait()
        send_on(0, i)
        return carry

    lax.fori_loop(0, NCH, take_psi, 0)

    diag = lax.broadcasted_iota(jnp.int32, (part, LANES), 0)
    diag_lane = lax.broadcasted_iota(jnp.int32, (part, LANES), 1)

    def take_tile(i, carry):
        pltpu.make_async_copy(tile, tiles.at[i], til_r.at[i]).wait()
        row = jnp.broadcast_to(tiles[i, 0:1, :], (part, LANES))
        d = jnp.sum(jnp.where(diag_lane == diag, row, 0.0), axis=1, keepdims=True)
        c = jnp.sum(jnp.where(diag_lane == diag + part, row, 0.0), axis=1, keepdims=True)
        dmp[chunk(i), :] = jnp.broadcast_to(d, (part, LANES))
        cen[chunk(i), :] = jnp.broadcast_to(c, (part, LANES))
        return carry

    lax.fori_loop(0, NCH, take_tile, 0)
    ce[...] = jnp.where(k_me < 2 * ZS - 1, tiles[0], 0.0)
    remote(ce, cp, cp_s, cp_r, above).start()

    fw[0] = jnp.zeros((rows, nang), F32)
    fw[1] = pb[0].astype(F32)

    def take_pot(s, carry):
        j = (v_me % 8 + 8 - s) % 8
        i = 2 * j + core
        pltpu.make_async_copy(pstage.at[0], pot.at[chunk(i), :], pot_r.at[j]).wait()
        remote(
            pot.at[chunk(i), :], pot.at[chunk(i), :], sib_s.at[j], sib_r.at[j], sibling
        ).start()
        return carry

    lax.fori_loop(0, NCH // 2, take_pot, 0)
    for load in loads:
        load.wait()

    def take_sib(j, carry):
        i = 2 * j + 1 - core
        pltpu.make_async_copy(pstage.at[0], pot.at[chunk(i), :], sib_r.at[j]).wait()
        return carry

    lax.fori_loop(0, NCH // 2, take_sib, 0)
    remote(ce, cp, cp_s, cp_r, above).wait()

    wide_q = 256

    def step(n, carry):
        for q in range(nquad // wide_q):
            cols = slice(q * wide_q, (q + 1) * wide_q)
            grid = jnp.dot(pb[n], basis[:, cols], preferred_element_type=F32)
            scaled[:, cols] = (grid * pot[:, cols].astype(F32)).astype(BF16)
        for q in range(nang // wide_q):
            cols = slice(q * wide_q, (q + 1) * wide_q)
            tot[:, cols] = jnp.dot(
                kin[...], pb[n, :, cols], preferred_element_type=F32
            ) + lax.dot_general(
                scaled[...],
                basis[cols, :],
                (((1,), (1,)), ((), ())),
                preferred_element_type=F32,
            )
        gain = jnp.where(n == 0, 1.0, 2.0).astype(F32)

        def finish(s, carry):
            i = order(s)
            pltpu.make_async_copy(stage.at[0], lo.at[n, chunk(i), :], lo_r.at[n, i]).wait()
            pltpu.make_async_copy(stage.at[0], up.at[n, chunk(i), :], up_r.at[n, i]).wait()
            d = dmp[chunk(i), :]
            c = cen[chunk(i), :]
            for b in range(nang // LANES):
                cols = slice(b * LANES, (b + 1) * LANES)
                h = (
                    tot[chunk(i), cols]
                    + c * fw[n + 1, chunk(i), cols]
                    + ce[2 + b : 3 + b, :] * up[n, chunk(i), cols].astype(F32)
                    + cp[2 + b : 3 + b, :] * lo[n, chunk(i), cols].astype(F32)
                )
                new = d * (gain * h - d * fw[n, chunk(i), cols])
                fw[n + 2, chunk(i), cols] = new
                pb[n + 1, chunk(i), cols] = new.astype(BF16)

            @pl.when(n < ITERS - 1)
            def _():
                send_on(n + 1, i)

            @pl.when(n == ITERS - 1)
            def _():
                push(
                    fw.at[ITERS + 1, chunk(i), :],
                    fin_ref.at[v_me],
                    fin_s.at[i],
                    fin_r.at[v_me],
                    (k_me, i),
                )

            return carry

        lax.fori_loop(0, NCH, finish, 0)
        return carry

    lax.fori_loop(0, ITERS, step, 0)

    radial = lax.broadcasted_iota(jnp.int32, (rows, LANES), 0)
    for b in range(crad_ref.shape[0]):
        hits = lax.dot_general(
            pb[ITERS],
            proj[b * LANES : (b + 1) * LANES, :],
            (((1,), (1,)), ((), ())),
            preferred_element_type=F32,
        )
        want = jnp.where(cvib_ref[b : b + 1, :] == v_me, crad_ref[b : b + 1, :], -1)
        chosen = jnp.where(radial == want, hits, 0.0)
        asend[b] = jnp.broadcast_to(jnp.sum(chosen, axis=0, keepdims=True), (8, LANES))

    def send_amp(s, carry):
        i = order(s)
        push(asend.at[i // 2], arecv.at[v_me], amp_s.at[i], amp_r.at[v_me], (k_me, i))
        return carry

    lax.fori_loop(0, NCH, send_amp, 0)

    def take_amp(v, carry):
        pltpu.make_async_copy(tile, arecv.at[v], amp_r.at[v]).wait()
        return carry + arecv[v]

    total = lax.fori_loop(0, NCH, take_amp, jnp.zeros((8, LANES), F32))
    half = amp_ref.shape[1]
    amp_ref[...] = jnp.where(rad % 2 == 1, total[0:1, half:], total[0:1, :half])

    def settle(s, carry):
        pltpu.make_async_copy(fin_ref.at[s], fin_ref.at[s], fin_r.at[s]).wait()
        v, device = holder(s)
        pushed(stage.at[v], pb.at[0, chunk(rad), :], psi_s.at[s], psi_r.at[rad], device)
        pushed(tile, tiles.at[rad], til_s.at[s], til_r.at[rad], device)
        i = order(s)
        pushed(
            fw.at[ITERS + 1, chunk(i), :], fin_ref.at[v_me], fin_s.at[i], fin_r.at[v_me], (k_me, i)
        )
        pushed(asend.at[i // 2], arecv.at[v_me], amp_s.at[i], amp_r.at[v_me], (k_me, i))
        return carry

    lax.fori_loop(0, NCH, settle, 0)

    def settle_halo(n, carry):
        def one(i, carry):
            part_n = pb.at[n, chunk(i), :]
            remote(part_n, lo.at[n, chunk(i), :], lo_s.at[n, i], lo_r.at[n, i], above).wait_send()
            remote(part_n, up.at[n, chunk(i), :], up_s.at[n, i], up_r.at[n, i], below).wait_send()
            return carry

        return lax.fori_loop(0, NCH, one, carry)

    lax.fori_loop(0, ITERS, settle_halo, 0)

    def settle_pot(s, carry):
        i, device = pot_holder(s)
        pushed(pstage.at[i], pot.at[chunk(rad), :], pot_s.at[s], pot_r.at[rad // 2], device)
        c = 2 * s + core
        remote(
            pot.at[chunk(c), :], pot.at[chunk(c), :], sib_s.at[s], sib_r.at[s], sibling
        ).wait_send()
        return carry

    lax.fori_loop(0, NCH // 2, settle_pot, 0)


def per_device(
    psi_start,
    potential,
    basis,
    kinetic,
    radial_factor,
    damping,
    coupling,
    helicity,
    chan_rad,
    chan_vib,
    projector,
):
    _, rdev, nvib, nang = psi_start.shape
    nquad = basis.shape[1]
    nchan = projector.shape[0]
    rows = NCH * rdev
    out_chan = nchan // NCH
    anyspace = pl.BlockSpec(memory_space=pl.ANY)
    smem = pl.BlockSpec(memory_space=pltpu.SMEM)
    vmem = pl.BlockSpec(memory_space=pltpu.VMEM)
    dma = pltpu.SemaphoreType.DMA
    fin, amp = pl.pallas_call(
        kernel,
        name="propagate",
        out_shape=(
            jax.ShapeDtypeStruct((nvib, rdev, nang), F32),
            jax.ShapeDtypeStruct((1, out_chan), F32),
        ),
        in_specs=[anyspace] * 5 + [smem] * 3 + [vmem] * 3,
        out_specs=(anyspace, vmem),
        scratch_shapes=[
            pltpu.VMEM((nang // LANES, rdev * nvib, LANES), F32),
            pltpu.VMEM((nquad // LANES, rdev * nvib, LANES), F32),
            pltpu.VMEM((nang, nquad), BF16),
            pltpu.VMEM((rows, rows), BF16),
            pltpu.VMEM((nchan, nang), BF16),
            pltpu.VMEM((nvib, rdev, nang), BF16),
            pltpu.VMEM((nvib // 2, rdev, nquad), BF16),
            pltpu.VMEM((8, LANES), F32),
            pltpu.VMEM((NCH, 8, LANES), F32),
            pltpu.VMEM((8, LANES), F32),
            pltpu.VMEM((8, LANES), F32),
            pltpu.VMEM((ITERS + 1, rows, nang), BF16),
            pltpu.VMEM((ITERS, rows, nang), BF16),
            pltpu.VMEM((ITERS, rows, nang), BF16),
            pltpu.VMEM((ITERS + 2, rows, nang), F32),
            pltpu.VMEM((rows, nquad), BF16),
            pltpu.VMEM((rows, nquad), BF16),
            pltpu.VMEM((rows, nang), F32),
            pltpu.VMEM((rows, LANES), F32),
            pltpu.VMEM((rows, LANES), F32),
            pltpu.VMEM((nchan // LANES, 8, LANES), F32),
            pltpu.VMEM((NCH, 8, LANES), F32),
            dma((3,)),
            dma((nang // LANES,)),
            dma((nquad // LANES,)),
            dma((NCH,)),
            dma((NCH,)),
            dma((NCH,)),
            dma((NCH,)),
            dma((NCH // 2,)),
            dma((NCH // 2,)),
            dma((NCH // 2,)),
            dma((NCH // 2,)),
            dma((ITERS, NCH)),
            dma((ITERS, NCH)),
            dma((ITERS, NCH)),
            dma((ITERS, NCH)),
            dma,
            dma,
            dma((NCH,)),
            dma((NCH,)),
            dma((NCH,)),
            dma((NCH,)),
        ],
        compiler_params=pltpu.CompilerParams(
            collective_id=0, has_side_effects=True, vmem_limit_bytes=56 * 2**20
        ),
    )(
        psi_start.reshape(rdev * nvib, nang),
        potential.reshape(rdev * nvib, nquad),
        basis,
        kinetic,
        projector,
        radial_factor,
        damping,
        helicity,
        coupling,
        chan_rad.reshape(-1, LANES),
        chan_vib.reshape(-1, LANES),
    )
    return (jnp.transpose(fin, (1, 0, 2))[None], amp)


def solution(mesh):
    placed = (
        P("hel", "rad", None, None),
        P("rad", None, None),
        P(),
        P(),
        P("rad"),
        P("rad"),
        P("hel", None),
        P("hel"),
        P(),
        P(),
        P(),
    )
    return jax.shard_map(
        per_device,
        mesh=mesh,
        in_specs=placed,
        out_specs=(P("hel", "rad", None, None), P("hel", "rad")),
        check_vma=False,
    )
```

time: 139 us -> 65 us (0.47)
  the two profiles are of different devices: /device:TPU:4 before, /device:TPU:1 now
where the time goes in v2:
time: 65 us; the launch traced here: 64.9 us
  Pallas kernels  60.6 us (93%)
  local copies, waits for them, and re-layouts  2.99 us (5%)
  between operations  1.3 us (2%)
    pallas_call x1, Pallas kernels, per_device(): pl.pallas_call(kernel, name='propagate', out_shape=(jax.ShapeDtypeStruct(...  60.6 us
    unnamed x4, local copies, waits for them, and re-layouts  2.99 us

profile of v2, /device:TPU:1, one launch (start us, length us, event | category | flops | bytes accessed | tf_op | source)
XLA Modules:
  0.0 64.9 jit_solution(17934337520180456838)
XLA Ops:
  1.3 60.6 %propagate.1 = (f32[16,16,768]{2,1,0:T(8,128)}, f32[1,64]{1,0:T(1,128)}) custom-call(f32[256,768]{1,0:T(8,128)} %bitcast.9, f32[256,1536]{1,0:T(8,128)} %bitcast.7, bf16[768,1536]{1,0:T(8,128)(2,1)} %basis_hbm.1, bf16[256,256]{1,0:T(8,128)(2,1)} %kin_hbm.1, bf16[1024,768]{1,0:T(8,128)(2,1)} %proj_hbm.1, f32[16]{0:T(128)} %rf_s.1, f32[16]{0:T(128)} %damp_s.1, ...), custom_call_target="tpu_custom_call" | custom-call | tf_op jit(solution)/shard_map/propagate/pallas_call | solution.py:416
  61.9 0.0 copy-start
  61.9 2.5 %copy.13 = f32[1,16,16,768]{3,2,1,0:T(8,128)} copy(f32[1,16,16,768]{3,1,2,0:T(8,128)} %bitcast.8) | data formatting | bytes 1572864
  64.4 0.0 copy-done
  64.4 0.5 copy.16
Async XLA Ops:
  61.9 2.5 %copy-start = (f32[1,64]{1,0:T(1,128)S(1)}, f32[1,64]{1,0:T(1,128)}, u32[]{:S(2)}) copy-start(f32[1,64]{1,0:T(1,128)} %get-tuple-element.11) | copy-start | bytes 772

commit v3 on v2

v3 whole, which is shorter than its diff:
```python
import jax
import jax.numpy as jnp
from jax import lax
from jax.experimental import pallas as pl
from jax.experimental.pallas import tpu as pltpu
from jax.sharding import PartitionSpec as P

ITERS = 3
MESH = pl.DeviceIdType.MESH
F32 = jnp.float32
BF16 = jnp.bfloat16
NCH = 16
ZS = 8
LANES = 128


def div(a, b):
    return lax.div(a, jnp.int32(b))


def rem(a, b):
    return lax.rem(a, jnp.int32(b))


def kernel(
    psi_hbm,
    pot_hbm,
    basis_hbm,
    kin_hbm,
    proj_hbm,
    rf_hbm,
    damp_hbm,
    hel_hbm,
    coup_hbm,
    crad_hbm,
    cvib_hbm,
    fin_ref,
    amp_ref,
    rf_ref,
    damp_ref,
    hel_ref,
    coup_ref,
    crad_ref,
    cvib_ref,
    psi_v,
    pot_v,
    basis,
    kin,
    proj,
    stage,
    pstage,
    tile,
    tiles,
    ce,
    cp,
    pb,
    late,
    lo,
    up,
    fw,
    pot,
    scaled,
    tot,
    dmp,
    cen,
    asend,
    arecv,
    kept,
    kept_sem,
    load_sem,
    psi_l,
    pot_l,
    psi_s,
    psi_r,
    til_s,
    til_r,
    pot_s,
    pot_r,
    sib_s,
    sib_r,
    lo_s,
    lo_r,
    up_s,
    up_r,
    cp_s,
    cp_r,
    fin_s,
    fin_r,
    amp_s,
    amp_r,
):
    hel, rad = lax.axis_index("hel"), lax.axis_index("rad")
    x_hi, z = div(hel, ZS), rem(hel, ZS)
    x_lo, y, core = div(rad, 8), rem(div(rad, 2), 4), rem(rad, 2)
    v_me = x_hi * 8 + x_lo * 4 + y
    k_me = core * ZS + z
    column = x_lo * 8 + y * 2
    z_up, z_down = rem(z + 1, ZS), rem(z + ZS - 1, ZS)
    above = (x_hi * ZS + z_up, column + rem(core + div(z + 1, ZS), 2))
    below = (x_hi * ZS + z_down, column + rem(core + 1 - div(z + ZS - 1, ZS), 2))
    sibling = (hel, column + 1 - core)
    rows, nang = pb.shape[1:]
    nquad = pot.shape[1]
    part = rows // NCH

    barrier = pltpu.get_barrier_semaphore()
    for neighbour in (above, below):
        pl.semaphore_signal(barrier, inc=1, device_id=neighbour, device_id_type=MESH)
    def greet(i, carry):
        pl.semaphore_signal(
            barrier, inc=1, device_id=((1 - x_hi) * ZS + z, i), device_id_type=MESH
        )

        @pl.when(i != rad)
        def _():
            pl.semaphore_signal(barrier, inc=1, device_id=(hel, i), device_id_type=MESH)

        return carry

    lax.fori_loop(0, NCH, greet, 0)

    def load_lanes(b, carry):
        cols = pl.ds(pl.multiple_of(b * LANES, LANES), LANES)
        pltpu.make_async_copy(psi_hbm.at[:, cols], psi_v.at[b], psi_l.at[b]).start()
        return carry

    def load_pot_lanes(b, carry):
        cols = pl.ds(pl.multiple_of(b * LANES, LANES), LANES)
        pltpu.make_async_copy(pot_hbm.at[:, cols], pot_v.at[b], pot_l.at[b]).start()
        return carry

    loads = [
        pltpu.make_async_copy(src, dst, load_sem.at[i])
        for i, (src, dst) in enumerate(
            [
                (rf_hbm, rf_ref),
                (damp_hbm, damp_ref),
                (hel_hbm, hel_ref),
                (coup_hbm, coup_ref),
                (kin_hbm, kin),
                (basis_hbm, basis),
                (proj_hbm, proj),
                (crad_hbm, crad_ref),
                (cvib_hbm, cvib_ref),
            ]
        )
    ]
    small_loads, big_loads = loads[:4], loads[4:]
    lax.fori_loop(0, nang // LANES, load_lanes, 0)
    for load in small_loads:
        load.start()
    lax.fori_loop(0, nquad // LANES, load_pot_lanes, 0)
    for load in big_loads:
        load.start()

    def chunk(i):
        return pl.ds(pl.multiple_of(i * part, part), part)

    def remote(src, dst, send, recv, device):
        return pltpu.make_async_remote_copy(
            src_ref=src,
            dst_ref=dst,
            send_sem=send,
            recv_sem=recv,
            device_id=device,
            device_id_type=MESH,
        )

    def is_here(device):
        return (device[0] == hel) & (device[1] == rad)

    def push(src, dst, send, recv, device):
        mine = is_here(device)

        @pl.when(mine)
        def _():
            pltpu.make_async_copy(src, dst, recv).start()

        @pl.when(jnp.logical_not(mine))
        def _():
            remote(src, dst, send, recv, device).start()

    def pushed(src, dst, send, recv, device):
        @pl.when(jnp.logical_not(is_here(device)))
        def _():
            remote(src, dst, send, recv, device).wait_send()

    for load in small_loads:
        load.wait()
    kvalue = hel_ref[...].astype(F32)
    tile[0:1, 0:part] = damp_ref[...]
    tile[1:2, 0:part] = -2.0 * (kvalue * kvalue) * rf_ref[...]
    wide = coup_ref[...].astype(F32)
    for b in range(nang // LANES):
        tile[2 + b : 3 + b, :] = wide[:, b * LANES : (b + 1) * LANES]

    for b in range(nang // LANES):
        cols = slice(b * LANES, (b + 1) * LANES)
        pltpu.make_async_copy(psi_hbm.at[:, cols], psi_v.at[b], psi_l.at[b]).wait()
        for v in range(NCH):
            stage[v, :, cols] = psi_v[b, pl.ds(v, part, stride=NCH), :].astype(BF16)
    pl.semaphore_wait(barrier, 2 * NCH + 1)

    def holder(s):
        v = rem(rad + s, NCH)
        return v, (div(v, 8) * ZS + z, rem(v, 8) * 2 + x_hi)

    def send_psi(s, carry):
        v, device = holder(s)
        push(stage.at[v], pb.at[0, chunk(rad), :], psi_s.at[s], psi_r.at[rad], device)
        return carry

    def send_tile(s, carry):
        v, device = holder(s)
        push(tile, tiles.at[rad], til_s.at[s], til_r.at[rad], device)
        return carry

    lax.fori_loop(0, NCH, send_tile, 0)
    lax.fori_loop(0, NCH, send_psi, 0)

    for b in range(nquad // LANES):
        cols = slice(b * LANES, (b + 1) * LANES)
        pltpu.make_async_copy(pot_hbm.at[:, cols], pot_v.at[b], pot_l.at[b]).wait()
        for i in range(NCH // 2):
            pstage[i, :, cols] = pot_v[b, pl.ds(x_hi * 8 + i, part, stride=NCH), :].astype(BF16)

    half_me = div(rad, 2)

    def pot_holder(s):
        i = rem(half_me + s, 8)
        return i, (hel, 2 * i + core)

    def send_pot(s, carry):
        i, device = pot_holder(s)
        push(pstage.at[i], pot.at[chunk(rad), :], pot_s.at[s], pot_r.at[half_me], device)
        return carry


    lax.fori_loop(0, NCH // 2, send_pot, 0)

    def send_on(n, i):
        remote(
            pb.at[n, chunk(i), :], lo.at[n, chunk(i), :], lo_s.at[n, i], lo_r.at[n, i], above
        ).start()
        remote(
            pb.at[n, chunk(i), :], up.at[n, chunk(i), :], up_s.at[n, i], up_r.at[n, i], below
        ).start()

    def order(s):
        return rem(v_me + NCH - s, NCH)

    def take_psi(s, carry):
        i = order(s)
        pltpu.make_async_copy(stage.at[0], pb.at[0, chunk(i), :], psi_r.at[i]).wait()
        send_on(0, i)
        return carry

    first = order(0)
    pltpu.make_async_copy(tile, tiles.at[first], til_r.at[first]).wait()
    ce[...] = jnp.where(k_me < 2 * ZS - 1, tiles[first], 0.0)
    remote(ce, cp, cp_s, cp_r, above).start()
    lax.fori_loop(0, NCH, take_psi, 0)

    diag = lax.broadcasted_iota(jnp.int32, (part, LANES), 0)
    diag_lane = lax.broadcasted_iota(jnp.int32, (part, LANES), 1)

    def take_pot(s, carry):
        j = rem(half_me + 8 - s, 8)
        i = 2 * j + core
        pltpu.make_async_copy(pstage.at[0], pot.at[chunk(i), :], pot_r.at[j]).wait()
        remote(
            pot.at[chunk(i), :], pot.at[chunk(i), :], sib_s.at[j], sib_r.at[j], sibling
        ).start()
        return carry

    lax.fori_loop(0, NCH // 2, take_pot, 0)

    def take_tile(s, carry):
        i = order(s)
        pltpu.make_async_copy(tile, tiles.at[i], til_r.at[i]).wait()
        return carry

    lax.fori_loop(1, NCH, take_tile, 0)
    for i in range(NCH):
        span = slice(i * part, (i + 1) * part)
        here = diag_lane == diag
        d_row = jnp.broadcast_to(tiles[i, 0:1, :], (part, LANES))
        c_row = jnp.broadcast_to(tiles[i, 1:2, :], (part, LANES))
        d = jnp.sum(jnp.where(here, d_row, 0.0), axis=1, keepdims=True)
        c = jnp.sum(jnp.where(here, c_row, 0.0), axis=1, keepdims=True)
        dmp[span, :] = jnp.broadcast_to(d, (part, LANES))
        cen[span, :] = jnp.broadcast_to(c, (part, LANES))
    asend[...] = jnp.zeros(asend.shape, F32)
    fw[0] = jnp.zeros((rows, nang), F32)
    fw[1] = pb[0].astype(F32)
    for load in big_loads:
        load.wait()

    def take_sib(j, carry):
        i = 2 * j + 1 - core
        pltpu.make_async_copy(pstage.at[0], pot.at[chunk(i), :], sib_r.at[j]).wait()
        return carry

    lax.fori_loop(0, NCH // 2, take_sib, 0)

    def settle_halo(n, i, carry):
        part_n = pb.at[n, chunk(i), :]
        remote(part_n, lo.at[n, chunk(i), :], lo_s.at[n, i], lo_r.at[n, i], above).wait_send()
        remote(part_n, up.at[n, chunk(i), :], up_s.at[n, i], up_r.at[n, i], below).wait_send()
        return carry

    def settle_in(s, carry):
        v, device = holder(s)
        pushed(stage.at[v], pb.at[0, chunk(rad), :], psi_s.at[s], psi_r.at[rad], device)
        pushed(tile, tiles.at[rad], til_s.at[s], til_r.at[rad], device)
        return carry

    def settle_pot(s, carry):
        i, device = pot_holder(s)
        pushed(pstage.at[i], pot.at[chunk(rad), :], pot_s.at[s], pot_r.at[half_me], device)
        c = 2 * s + core
        remote(
            pot.at[chunk(c), :], pot.at[chunk(c), :], sib_s.at[s], sib_r.at[s], sibling
        ).wait_send()
        return carry

    wide_q = 256

    group = 4
    grows = group * part
    in_group = lax.broadcasted_iota(jnp.int32, (grows, LANES), 0)

    def project(g):
        radial = rem(v_me + NCH - g * group - div(in_group, part), NCH) * part + rem(in_group, part)
        block = late[pl.ds(pl.multiple_of(g * grows, grows), grows), :]
        for b in range(0, crad_ref.shape[0], 2):
            hits = lax.dot_general(
                block,
                proj[b * LANES : (b + 2) * LANES, :],
                (((1,), (1,)), ((), ())),
                preferred_element_type=F32,
            )
            for h in range(2):
                line = slice(b + h, b + h + 1)
                want = jnp.where(cvib_ref[line, :] == v_me, crad_ref[line, :], -1)
                chosen = jnp.where(radial == want, hits[:, h * LANES : (h + 1) * LANES], 0.0)
                asend[b + h] += jnp.broadcast_to(
                    jnp.sum(chosen, axis=0, keepdims=True), (8, LANES)
                )

    def step(n, carry):
        for q in range(nquad // wide_q):
            cols = slice(q * wide_q, (q + 1) * wide_q)
            grid = jnp.dot(pb[n], basis[:, cols], preferred_element_type=F32)
            scaled[:, cols] = (grid * pot[:, cols].astype(F32)).astype(BF16)
        for q in range(nang // wide_q):
            cols = slice(q * wide_q, (q + 1) * wide_q)
            tot[:, cols] = jnp.dot(
                kin[...], pb[n, :, cols], preferred_element_type=F32
            ) + lax.dot_general(
                scaled[...],
                basis[cols, :],
                (((1,), (1,)), ((), ())),
                preferred_element_type=F32,
            )

        @pl.when(n == 1)
        def _():
            lax.fori_loop(0, NCH, settle_in, 0)
            lax.fori_loop(0, NCH // 2, settle_pot, 0)

        @pl.when(n >= 1)
        def _():
            lax.fori_loop(0, NCH, lambda i, c: settle_halo(n - 1, i, c), 0)

        @pl.when(n == 0)
        def _():
            remote(ce, cp, cp_s, cp_r, above).wait()

        spare = pltpu.make_async_copy(fw.at[n + 1, 0:8, 0:LANES], kept, kept_sem)
        spare.start()
        spare.wait()
        gain = jnp.where(n == 0, 1.0, 2.0).astype(F32)

        def finish(s, carry):
            i = order(s)
            pltpu.make_async_copy(stage.at[0], lo.at[n, chunk(i), :], lo_r.at[n, i]).wait()
            pltpu.make_async_copy(stage.at[0], up.at[n, chunk(i), :], up_r.at[n, i]).wait()
            d = dmp[chunk(i), :]
            c = cen[chunk(i), :]
            for b in range(nang // LANES):
                cols = slice(b * LANES, (b + 1) * LANES)
                h = (
                    tot[chunk(i), cols]
                    + c * fw[n + 1, chunk(i), cols]
                    + ce[2 + b : 3 + b, :] * up[n, chunk(i), cols].astype(F32)
                    + cp[2 + b : 3 + b, :] * lo[n, chunk(i), cols].astype(F32)
                )
                new = d * (gain * h - d * fw[n, chunk(i), cols])
                fw[n + 2, chunk(i), cols] = new
                pb[n + 1, chunk(i), cols] = new.astype(BF16)

            late[chunk(s), :] = pb[n + 1, chunk(i), :]

            @pl.when(n < ITERS - 1)
            def _():
                send_on(n + 1, i)

            @pl.when(n == ITERS - 1)
            def _():
                push(
                    pb.at[ITERS, chunk(i), :],
                    fin_ref.at[v_me],
                    fin_s.at[i],
                    fin_r.at[v_me],
                    (k_me, i),
                )

                @pl.when(rem(s, group) == group - 1)
                def _():
                    project(div(s, group))

            return carry

        lax.fori_loop(0, NCH, finish, 0)
        return carry

    lax.fori_loop(0, ITERS, step, 0)

    def send_amp(s, carry):
        i = order(s)
        push(asend.at[div(i, 2)], arecv.at[v_me], amp_s.at[i], amp_r.at[v_me], (k_me, i))
        return carry

    lax.fori_loop(0, NCH, send_amp, 0)

    def settle(s, carry):
        i = order(s)
        settle_halo(ITERS - 1, s, carry)
        pushed(
            pb.at[ITERS, chunk(i), :], fin_ref.at[v_me], fin_s.at[i], fin_r.at[v_me], (k_me, i)
        )
        pushed(asend.at[div(i, 2)], arecv.at[v_me], amp_s.at[i], amp_r.at[v_me], (k_me, i))
        return carry

    lax.fori_loop(0, NCH, settle, 0)

    def take_fin(v, carry):
        pltpu.make_async_copy(stage.at[0], fin_ref.at[v], fin_r.at[v]).wait()
        return carry

    lax.fori_loop(0, NCH, take_fin, 0)
    for v in range(NCH):
        pltpu.make_async_copy(tile, arecv.at[v], amp_r.at[v]).wait()
    amp_ref[...] = jnp.sum(arecv[...], axis=0)


def place(fin_hbm, amp_ref, out_hbm, half_ref, fin, out, sem, out_sem):
    load = pltpu.make_async_copy(fin_hbm, fin, sem)
    load.start()
    rad = lax.axis_index("rad")
    half = half_ref.shape[1]
    half_ref[...] = jnp.where(rad % 2 == 1, amp_ref[0:1, half:], amp_ref[0:1, :half])
    nvib, part, nang = fin.shape
    load.wait()
    copies = []
    for b in range(nang // LANES):
        cols = slice(b * LANES, (b + 1) * LANES)
        for v in range(nvib):
            out[b, pl.ds(v, part, stride=nvib), :] = fin[v, :, cols].astype(F32)
        copies.append(pltpu.make_async_copy(out.at[b], out_hbm.at[:, cols], out_sem.at[b]))
        copies[-1].start()
    for copy in copies:
        copy.wait()


def per_device(
    psi_start,
    potential,
    basis,
    kinetic,
    radial_factor,
    damping,
    coupling,
    helicity,
    chan_rad,
    chan_vib,
    projector,
):
    _, rdev, nvib, nang = psi_start.shape
    nquad = basis.shape[1]
    nchan = projector.shape[0]
    rows = NCH * rdev
    out_chan = nchan // NCH
    anyspace = pl.BlockSpec(memory_space=pl.ANY)
    vmem = pl.BlockSpec(memory_space=pltpu.VMEM)
    dma = pltpu.SemaphoreType.DMA
    fin, amp = pl.pallas_call(
        kernel,
        name="propagate",
        out_shape=(
            jax.ShapeDtypeStruct((nvib, rdev, nang), BF16),
            jax.ShapeDtypeStruct((8, LANES), F32),
        ),
        in_specs=[anyspace] * 11,
        out_specs=(anyspace, vmem),
        scratch_shapes=[
            pltpu.VMEM((1, rdev), F32),
            pltpu.VMEM((1, rdev), F32),
            pltpu.VMEM((1, 1), jnp.int32),
            pltpu.VMEM((1, nang), BF16),
            pltpu.VMEM((nchan // LANES, LANES), jnp.int32),
            pltpu.VMEM((nchan // LANES, LANES), jnp.int32),
            pltpu.VMEM((nang // LANES, rdev * nvib, LANES), F32),
            pltpu.VMEM((nquad // LANES, rdev * nvib, LANES), F32),
            pltpu.VMEM((nang, nquad), BF16),
            pltpu.VMEM((rows, rows), BF16),
            pltpu.VMEM((nchan, nang), BF16),
            pltpu.VMEM((nvib, rdev, nang), BF16),
            pltpu.VMEM((nvib // 2, rdev, nquad), BF16),
            pltpu.VMEM((8, LANES), F32),
            pltpu.VMEM((NCH, 8, LANES), F32),
            pltpu.VMEM((8, LANES), F32),
            pltpu.VMEM((8, LANES), F32),
            pltpu.VMEM((ITERS + 1, rows, nang), BF16),
            pltpu.VMEM((rows, nang), BF16),
            pltpu.VMEM((ITERS, rows, nang), BF16),
            pltpu.VMEM((ITERS, rows, nang), BF16),
            pltpu.VMEM((ITERS + 2, rows, nang), F32),
            pltpu.VMEM((rows, nquad), BF16),
            pltpu.VMEM((rows, nquad), BF16),
            pltpu.VMEM((rows, nang), F32),
            pltpu.VMEM((rows, LANES), F32),
            pltpu.VMEM((rows, LANES), F32),
            pltpu.VMEM((nchan // LANES, 8, LANES), F32),
            pltpu.VMEM((NCH, 8, LANES), F32),
            pltpu.VMEM((8, LANES), F32),
            dma,
            dma((9,)),
            dma((nang // LANES,)),
            dma((nquad // LANES,)),
            dma((NCH,)),
            dma((NCH,)),
            dma((NCH,)),
            dma((NCH,)),
            dma((NCH // 2,)),
            dma((NCH // 2,)),
            dma((NCH // 2,)),
            dma((NCH // 2,)),
            dma((ITERS, NCH)),
            dma((ITERS, NCH)),
            dma((ITERS, NCH)),
            dma((ITERS, NCH)),
            dma,
            dma,
            dma((NCH,)),
            dma((NCH,)),
            dma((NCH,)),
            dma((NCH,)),
        ],
        compiler_params=pltpu.CompilerParams(
            collective_id=0, has_side_effects=True, vmem_limit_bytes=56 * 2**20
        ),
    )(
        psi_start.reshape(rdev * nvib, nang),
        potential.reshape(rdev * nvib, nquad),
        basis,
        kinetic,
        projector,
        radial_factor.reshape(1, -1),
        damping.reshape(1, -1),
        helicity.reshape(1, 1),
        coupling,
        chan_rad.reshape(-1, LANES),
        chan_vib.reshape(-1, LANES),
    )
    psi_final, amplitude = pl.pallas_call(
        place,
        name="place",
        out_shape=(
            jax.ShapeDtypeStruct((rows, nang), F32),
            jax.ShapeDtypeStruct((1, out_chan), F32),
        ),
        in_specs=[anyspace, vmem],
        out_specs=(anyspace, vmem),
        scratch_shapes=[
            pltpu.VMEM((nvib, rdev, nang), BF16),
            pltpu.VMEM((nang // LANES, rows, LANES), F32),
            dma,
            dma((nang // LANES,)),
        ],
    )(fin, amp)
    return (psi_final.reshape(1, rdev, nvib, nang), amplitude)


def solution(mesh):
    placed = (
        P("hel", "rad", None, None),
        P("rad", None, None),
        P(),
        P(),
        P("rad"),
        P("rad"),
        P("hel", None),
        P("hel"),
        P(),
        P(),
        P(),
    )
    return jax.shard_map(
        per_device,
        mesh=mesh,
        in_specs=placed,
        out_specs=(P("hel", "rad", None, None), P("hel", "rad")),
        check_vma=False,
    )
```

time: 65 us -> 59.9 us (0.922)
  local copies, waits for them, and re-layouts: 2.99 us -> 0 us
  Pallas kernels: 60.6 us -> 58.5 us
    pallas_call x1, Pallas kernels: 60.6 us -> 55.3 us  [per_device(): pl.pallas_call(kernel, name='propagate', out_shape=(jax.ShapeDtypeStruct(...]
    pallas_call x0 -> x1, Pallas kernels: none -> 3.16 us  [per_device(): pl.pallas_call(place, name='place', out_shape=(jax.ShapeDtypeStruct((rows...]
    unnamed x4 -> x0, local copies, waits for them, and re-layouts: 2.99 us -> none
where the time goes in v3:
time: 59.9 us; the launch traced here: 59.8 us
  Pallas kernels  58.5 us (98%)
  between operations  1.29 us (2%)
    pallas_call x1, Pallas kernels, per_device(): pl.pallas_call(kernel, name='propagate', out_shape=(jax.ShapeDtypeStruct(...  55.3 us
    pallas_call x1, Pallas kernels, per_device(): pl.pallas_call(place, name='place', out_shape=(jax.ShapeDtypeStruct((rows...  3.16 us

profile of v3, /device:TPU:1, one launch (start us, length us, event | category | flops | bytes accessed | tf_op | source)
XLA Modules:
  0.0 59.8 jit_solution(15152306257062029127)
XLA Ops:
  1.3 55.3 %propagate.1 = (bf16[16,16,768]{2,1,0:T(8,128)(2,1)}, f32[8,128]{1,0:T(8,128)}) custom-call(f32[256,768]{1,0:T(8,128)} %bitcast.10, f32[256,1536]{1,0:T(8,128)} %bitcast.9, bf16[768,1536]{1,0:T(8,128)(2,1)} %basis_hbm.1, bf16[256,256]{1,0:T(8,128)(2,1)} %kin_hbm.1, bf16[1024,768]{1,0:T(8,128)(2,1)} %proj_hbm.1, f32[1,16]{1,0:T(1,128)} %bitcast.13, ...), custom_call_target="tpu_custom_call" | custom-call | tf_op jit(solution)/shard_map/propagate/pallas_call | solution.py:498
  56.6 3.2 %place.1 = (f32[256,768]{1,0:T(8,128)}, f32[1,64]{1,0:T(1,128)}) custom-call(bf16[16,16,768]{2,1,0:T(8,128)(2,1)} %get-tuple-element.6.fin_hbm, f32[8,128]{1,0:T(8,128)} %get-tuple-element.7.amp_ref), custom_call_target="tpu_custom_call" | custom-call | tf_op jit(solution)/shard_map/place/pallas_call | solution.py:577

commit v4 on v3

--- a/solution.py
+++ b/solution.py
@@ -65,8 +65,6 @@
     cen,
     asend,
     arecv,
-    kept,
-    kept_sem,
     load_sem,
     psi_l,
     pot_l,
@@ -364,23 +362,17 @@
                 preferred_element_type=F32,
             )
 
-        @pl.when(n == 1)
-        def _():
+        if n == 1:
             lax.fori_loop(0, NCH, settle_in, 0)
             lax.fori_loop(0, NCH // 2, settle_pot, 0)
 
-        @pl.when(n >= 1)
-        def _():
+        if n >= 1:
             lax.fori_loop(0, NCH, lambda i, c: settle_halo(n - 1, i, c), 0)
 
-        @pl.when(n == 0)
-        def _():
+        if n == 0:
             remote(ce, cp, cp_s, cp_r, above).wait()
 
-        spare = pltpu.make_async_copy(fw.at[n + 1, 0:8, 0:LANES], kept, kept_sem)
-        spare.start()
-        spare.wait()
-        gain = jnp.where(n == 0, 1.0, 2.0).astype(F32)
+        gain = 1.0 if n == 0 else 2.0
 
         def finish(s, carry):
             i = order(s)
@@ -400,14 +392,12 @@
                 fw[n + 2, chunk(i), cols] = new
                 pb[n + 1, chunk(i), cols] = new.astype(BF16)
 
-            late[chunk(s), :] = pb[n + 1, chunk(i), :]
-
-            @pl.when(n < ITERS - 1)
-            def _():
+            if n == ITERS - 1:
+                late[chunk(s), :] = pb[n + 1, chunk(i), :]
+
+            if n < ITERS - 1:
                 send_on(n + 1, i)
-
-            @pl.when(n == ITERS - 1)
-            def _():
+            else:
                 push(
                     pb.at[ITERS, chunk(i), :],
                     fin_ref.at[v_me],
@@ -425,7 +415,8 @@
         lax.fori_loop(0, NCH, finish, 0)
         return carry
 
-    lax.fori_loop(0, ITERS, step, 0)
+    for n in range(ITERS):
+        step(n, 0)
 
     def send_amp(s, carry):
         i = order(s)
@@ -534,8 +525,6 @@
             pltpu.VMEM((rows, LANES), F32),
             pltpu.VMEM((nchan // LANES, 8, LANES), F32),
             pltpu.VMEM((NCH, 8, LANES), F32),
-            pltpu.VMEM((8, LANES), F32),
-            dma,
             dma((9,)),
             dma((nang // LANES,)),
             dma((nquad // LANES,)),

time: 59.9 us -> 59.9 us (level)
  no operation moved by 1% of the time
where the time goes in v4:
time: 59.9 us; the launch traced here: 59.7 us
  Pallas kernels  58.4 us (97%)
  between operations  1.29 us (2%)
    pallas_call x1, Pallas kernels, per_device(): pl.pallas_call(kernel, name='propagate', out_shape=(jax.ShapeDtypeStruct(...  55.3 us
    pallas_call x1, Pallas kernels, per_device(): pl.pallas_call(place, name='place', out_shape=(jax.ShapeDtypeStruct((rows...  3.16 us

profile of v4, /device:TPU:1, one launch (start us, length us, event | category | flops | bytes accessed | tf_op | source)
XLA Modules:
  0.0 59.7 jit_solution(11389343499953079884)
XLA Ops:
  1.3 55.3 %propagate.1 = (bf16[16,16,768]{2,1,0:T(8,128)(2,1)}, f32[8,128]{1,0:T(8,128)}) custom-call(f32[256,768]{1,0:T(8,128)} %bitcast.10, f32[256,1536]{1,0:T(8,128)} %bitcast.9, bf16[768,1536]{1,0:T(8,128)(2,1)} %basis_hbm.1, bf16[256,256]{1,0:T(8,128)(2,1)} %kin_hbm.1, bf16[1024,768]{1,0:T(8,128)(2,1)} %proj_hbm.1, f32[1,16]{1,0:T(1,128)} %bitcast.13, ...), custom_call_target="tpu_custom_call" | custom-call | tf_op jit(solution)/shard_map/propagate/pallas_call | solution.py:489
  56.5 3.2 %place.1 = (f32[256,768]{1,0:T(8,128)}, f32[1,64]{1,0:T(1,128)}) custom-call(bf16[16,16,768]{2,1,0:T(8,128)(2,1)} %get-tuple-element.6.fin_hbm, f32[8,128]{1,0:T(8,128)} %get-tuple-element.7.amp_ref), custom_call_target="tpu_custom_call" | custom-call | tf_op jit(solution)/shard_map/place/pallas_call | solution.py:566
